TPU v7x, 256 devices: a whole 4x4x8 slice. The times are simulated.
256 devices in a mesh: slab: 16 (over x, y_lo, core), blk: 16 (over z, y_hi).
Axes of the slice: x: 4, y: 4 (y_hi: 2, y_lo: 2; y = y_hi * 2 + y_lo), z: 8, core: 2. Of those that a mesh axis runs over, the one named last changes fastest.
Arguments:
- queries: bfloat16 [8192, 768], P(('slab', 'blk')), may hold values from -6 to 6
- passages: bfloat16 [8192, 768], P(('blk', 'slab')), may hold values from -6 to 6
- query_lognorm: float32 [8192], P(('slab', 'blk')), as said below
- passage_lognorm: float32 [8192], P('blk'), as said below
- loss_cotangent: float32 [], replicated, may hold values from 4 to 12
Outputs:
- query_gradient: float32 [8192, 768], P(('slab', 'blk'))
- passage_gradient: float32 [8192, 768], P(('blk', 'slab'))
Inputs may be any that keep to these rules, and one draw needn't show every extreme that they name: `query_lognorm`: every entry lies between log(8192) + 0.5 and log(8192) + 3.5. `passage_lognorm`: every entry lies between log(8192) + 0.5 and log(8192) + 3.5.
All inputs are finite; a program needn't handle non-finite values.
Results may differ from a plain program's by a relative error of at most 0.034.
Values may be sent and summed in bfloat16 or wider, within the bound.
A program may use at most 64 MiB of HBM per device.

v0:
```python
import math

import jax
import jax.numpy as jnp
from jax import lax
from jax.sharding import PartitionSpec as P


def passed_along(block, axis, distance):
    devices = range(lax.axis_size(axis))
    route = [((i - distance) % len(devices), i) for i in devices]
    return lax.ppermute(block, axis, route)


def tile_gradients(
    query_rows,
    query_norms,
    row_numbers,
    passage_block,
    block_wide,
    block_norms,
    column_start,
    score_scale,
    half_cotangent,
):
    scores = score_scale * lax.dot_general(
        query_rows, passage_block, (((1,), (1,)), ((), ())), preferred_element_type=jnp.float32
    )
    column_numbers = column_start + lax.broadcasted_iota(jnp.int32, scores.shape, 1)
    paired = (row_numbers[:, None] == column_numbers).astype(jnp.float32)
    weights = half_cotangent * (
        jnp.exp(scores - query_norms[:, None])
        + jnp.exp(scores - block_norms[None, :])
        - 2.0 * paired
    )
    rows_wide = query_rows.astype(jnp.float32)
    query_term = score_scale * jnp.dot(
        weights, block_wide, precision=lax.Precision.HIGHEST, preferred_element_type=jnp.float32
    )
    passage_term = score_scale * lax.dot_general(
        weights,
        rows_wide,
        (((0,), (0,)), ((), ())),
        precision=lax.Precision.HIGHEST,
        preferred_element_type=jnp.float32,
    )
    return (query_term, passage_term)


def local(queries, passages, query_lognorm, passage_lognorm, loss_cotangent):
    per_device = queries.shape[0]
    feature_width = queries.shape[1]
    score_scale = 2.0 / math.sqrt(feature_width)
    half_cotangent = 0.5 * loss_cotangent
    cycle_count = lax.axis_size("blk")
    slab_index = lax.axis_index("slab")
    cycle_index = lax.axis_index("blk")
    passage_block = lax.all_gather(passages, "slab", axis=0, tiled=True)
    block_wide = passage_block.astype(jnp.float32)
    column_start = cycle_index * passage_block.shape[0]
    local_index = lax.broadcasted_iota(jnp.int32, (per_device,), 0)
    block_start = jnp.zeros(passage_block.shape, jnp.float32)

    def owner_offset(source_index):
        return (slab_index * cycle_count + source_index) * per_device

    def advance(cycle_turn, state_carry):
        query_rows, query_norms, carried_sum, block_total = state_carry
        source_index = (cycle_index - cycle_turn) % cycle_count
        query_term, passage_term = tile_gradients(
            query_rows,
            query_norms,
            owner_offset(source_index) + local_index,
            passage_block,
            block_wide,
            passage_lognorm,
            column_start,
            score_scale,
            half_cotangent,
        )
        query_rows = passed_along(query_rows, "blk", 1)
        query_norms, carried_sum = passed_along((query_norms, carried_sum + query_term), "blk", 1)
        return (query_rows, query_norms, carried_sum, block_total + passage_term)

    state_carry = (queries, query_lognorm, jnp.zeros(queries.shape, jnp.float32), block_start)
    state_carry = lax.fori_loop(0, cycle_count, advance, state_carry)
    query_gradient = state_carry[2]
    block_total = state_carry[3]
    passage_gradient = lax.psum_scatter(block_total, "slab", scatter_dimension=0, tiled=True)
    return (query_gradient, passage_gradient)


def solution(mesh):
    return jax.shard_map(
        local,
        mesh=mesh,
        in_specs=(
            P(("slab", "blk"), None),
            P(("blk", "slab"), None),
            P(("slab", "blk")),
            P("blk"),
            P(),
        ),
        out_specs=(P(("slab", "blk"), None), P(("blk", "slab"), None)),
        check_vma=False,
    )
```

profile of v0, /device:TPU:1, one launch (start us, length us, event | category | flops | bytes accessed | tf_op | source)
XLA Modules:
  0.0 328.0 jit_solution(9704652574744837015)
XLA Ops:
  7.9 23.4 %all_gather.3 = bf16[512,768]{1,0:T(8,128)(2,1)S(1)} all-gather(bf16[32,768]{1,0:T(8,128)(2,1)} %param.8), channel_id=1, replica_groups=mesh['slab'=16,'blk'=16] {'slab'}, dimensions={0}, use_global_device_ids=true | all-gather | bytes 835584 | tf_op jit(solution)/shard_map/all_gather | solution.py:58
  32.4 203.1 %while.22 = (s32[]{:T(128)}, bf16[32,768]{1,0:T(8,128)(2,1)S(1)}, f32[32]{0:T(128)S(1)}, f32[32,768]{1,0:T(8,128)S(1)}, f32[512,768]{1,0:T(8,128)S(1)}, /*index=...) while((s32[]{:T(128)}, bf16[32,768]{1,0:T(8,128)(2,1)S(1)}, ...), condition=%wide.region_1.2_spmd.clone, body=%wide.region_0.1_spmd.clone.sunk | while | flops 328516160 | bytes 6692412 | solution.py:86
  32.4 2.8 collective-permute-start.1
  39.4 2.7 collective-permute-start.2
  43.3 3.2 collective-permute-done.2
  47.1 2.6 collective-permute-start
  55.2 4.1 %collective-permute-done.2 = f32[32,768]{1,0:T(8,128)S(1)} collective-permute-done((f32[32,768]{1,0:T(8,128)S(1)}, f32[32,768]{1,0:T(8,128)S(1)}, u32[]{:S(2)}, u32[]{:S(2)}) %collective-permute-start.2) | collective-permute-done | bytes 98336 | tf_op jit(solution)/shard_map/while/body/eval_jaxpr/ppermute | solution.py:12
  59.4 3.1 collective-permute-start
  67.6 4.6 %collective-permute-done.2 = f32[32,768]{1,0:T(8,128)S(1)} collective-permute-done((f32[32,768]{1,0:T(8,128)S(1)}, f32[32,768]{1,0:T(8,128)S(1)}, u32[]{:S(2)}, u32[]{:S(2)}) %collective-permute-start.2) | collective-permute-done | bytes 98336 | tf_op jit(solution)/shard_map/while/body/eval_jaxpr/ppermute | solution.py:12
  72.3 4.2 %collective-permute-start = (bf16[32,768]{1,0:T(8,128)(2,1)S(1)}, bf16[32,768]{1,0:T(8,128)(2,1)S(1)}, u32[]{:S(2)}, u32[]{:S(2)}) collective-permute-start(bf16[32,768]{1,0:T(8,128)(2,1)S(1)} %copy.13), channel_id=1, source_target_pairs={{15,0},{0,1},{1,2},{2,3},{3,4},{4,5},{5,6},{6,7},{7,8},{8,9},{9,10... | collective-permute-start | bytes 147464 | tf_op jit(solution)/shard_map/while/body/eval_jaxpr/ppermute | solution.py:12
  80.7 5.5 %collective-permute-done.2 = f32[32,768]{1,0:T(8,128)S(1)} collective-permute-done((f32[32,768]{1,0:T(8,128)S(1)}, f32[32,768]{1,0:T(8,128)S(1)}, u32[]{:S(2)}, u32[]{:S(2)}) %collective-permute-start.2) | collective-permute-done | bytes 98336 | tf_op jit(solution)/shard_map/while/body/eval_jaxpr/ppermute | solution.py:12
  86.2 3.4 %collective-permute-start = (bf16[32,768]{1,0:T(8,128)(2,1)S(1)}, bf16[32,768]{1,0:T(8,128)(2,1)S(1)}, u32[]{:S(2)}, u32[]{:S(2)}) collective-permute-start(bf16[32,768]{1,0:T(8,128)(2,1)S(1)} %copy.13), channel_id=1, source_target_pairs={{15,0},{0,1},{1,2},{2,3},{3,4},{4,5},{5,6},{6,7},{7,8},{8,9},{9,10... | collective-permute-start | bytes 147464 | tf_op jit(solution)/shard_map/while/body/eval_jaxpr/ppermute | solution.py:12
  93.5 5.8 %collective-permute-done.2 = f32[32,768]{1,0:T(8,128)S(1)} collective-permute-done((f32[32,768]{1,0:T(8,128)S(1)}, f32[32,768]{1,0:T(8,128)S(1)}, u32[]{:S(2)}, u32[]{:S(2)}) %collective-permute-start.2) | collective-permute-done | bytes 98336 | tf_op jit(solution)/shard_map/while/body/eval_jaxpr/ppermute | solution.py:12
  99.3 2.6 collective-permute-start
  105.9 5.6 %collective-permute-done.2 = f32[32,768]{1,0:T(8,128)S(1)} collective-permute-done((f32[32,768]{1,0:T(8,128)S(1)}, f32[32,768]{1,0:T(8,128)S(1)}, u32[]{:S(2)}, u32[]{:S(2)}) %collective-permute-start.2) | collective-permute-done | bytes 98336 | tf_op jit(solution)/shard_map/while/body/eval_jaxpr/ppermute | solution.py:12
  111.5 2.2 collective-permute-start
  118.1 5.2 %collective-permute-done.2 = f32[32,768]{1,0:T(8,128)S(1)} collective-permute-done((f32[32,768]{1,0:T(8,128)S(1)}, f32[32,768]{1,0:T(8,128)S(1)}, u32[]{:S(2)}, u32[]{:S(2)}) %collective-permute-start.2) | collective-permute-done | bytes 98336 | tf_op jit(solution)/shard_map/while/body/eval_jaxpr/ppermute | solution.py:12
  130.0 5.6 %collective-permute-done.2 = f32[32,768]{1,0:T(8,128)S(1)} collective-permute-done((f32[32,768]{1,0:T(8,128)S(1)}, f32[32,768]{1,0:T(8,128)S(1)}, u32[]{:S(2)}, u32[]{:S(2)}) %collective-permute-start.2) | collective-permute-done | bytes 98336 | tf_op jit(solution)/shard_map/while/body/eval_jaxpr/ppermute | solution.py:12
  142.3 4.3 %collective-permute-done.2 = f32[32,768]{1,0:T(8,128)S(1)} collective-permute-done((f32[32,768]{1,0:T(8,128)S(1)}, f32[32,768]{1,0:T(8,128)S(1)}, u32[]{:S(2)}, u32[]{:S(2)}) %collective-permute-start.2) | collective-permute-done | bytes 98336 | tf_op jit(solution)/shard_map/while/body/eval_jaxpr/ppermute | solution.py:12
  146.6 2.5 collective-permute-start
  153.8 5.0 %collective-permute-done.2 = f32[32,768]{1,0:T(8,128)S(1)} collective-permute-done((f32[32,768]{1,0:T(8,128)S(1)}, f32[32,768]{1,0:T(8,128)S(1)}, u32[]{:S(2)}, u32[]{:S(2)}) %collective-permute-start.2) | collective-permute-done | bytes 98336 | tf_op jit(solution)/shard_map/while/body/eval_jaxpr/ppermute | solution.py:12
  158.8 4.2 %collective-permute-start = (bf16[32,768]{1,0:T(8,128)(2,1)S(1)}, bf16[32,768]{1,0:T(8,128)(2,1)S(1)}, u32[]{:S(2)}, u32[]{:S(2)}) collective-permute-start(bf16[32,768]{1,0:T(8,128)(2,1)S(1)} %copy.13), channel_id=1, source_target_pairs={{15,0},{0,1},{1,2},{2,3},{3,4},{4,5},{5,6},{6,7},{7,8},{8,9},{9,10... | collective-permute-start | bytes 147464 | tf_op jit(solution)/shard_map/while/body/eval_jaxpr/ppermute | solution.py:12
  166.9 5.8 %collective-permute-done.2 = f32[32,768]{1,0:T(8,128)S(1)} collective-permute-done((f32[32,768]{1,0:T(8,128)S(1)}, f32[32,768]{1,0:T(8,128)S(1)}, u32[]{:S(2)}, u32[]{:S(2)}) %collective-permute-start.2) | collective-permute-done | bytes 98336 | tf_op jit(solution)/shard_map/while/body/eval_jaxpr/ppermute | solution.py:12
  172.7 3.3 %collective-permute-start = (bf16[32,768]{1,0:T(8,128)(2,1)S(1)}, bf16[32,768]{1,0:T(8,128)(2,1)S(1)}, u32[]{:S(2)}, u32[]{:S(2)}) collective-permute-start(bf16[32,768]{1,0:T(8,128)(2,1)S(1)} %copy.13), channel_id=1, source_target_pairs={{15,0},{0,1},{1,2},{2,3},{3,4},{4,5},{5,6},{6,7},{7,8},{8,9},{9,10... | collective-permute-start | bytes 147464 | tf_op jit(solution)/shard_map/while/body/eval_jaxpr/ppermute | solution.py:12
  180.5 5.2 %collective-permute-done.2 = f32[32,768]{1,0:T(8,128)S(1)} collective-permute-done((f32[32,768]{1,0:T(8,128)S(1)}, f32[32,768]{1,0:T(8,128)S(1)}, u32[]{:S(2)}, u32[]{:S(2)}) %collective-permute-start.2) | collective-permute-done | bytes 98336 | tf_op jit(solution)/shard_map/while/body/eval_jaxpr/ppermute | solution.py:12
  185.7 3.7 %collective-permute-start = (bf16[32,768]{1,0:T(8,128)(2,1)S(1)}, bf16[32,768]{1,0:T(8,128)(2,1)S(1)}, u32[]{:S(2)}, u32[]{:S(2)}) collective-permute-start(bf16[32,768]{1,0:T(8,128)(2,1)S(1)} %copy.13), channel_id=1, source_target_pairs={{15,0},{0,1},{1,2},{2,3},{3,4},{4,5},{5,6},{6,7},{7,8},{8,9},{9,10... | collective-permute-start | bytes 147464 | tf_op jit(solution)/shard_map/while/body/eval_jaxpr/ppermute | solution.py:12
  193.3 5.8 %collective-permute-done.2 = f32[32,768]{1,0:T(8,128)S(1)} collective-permute-done((f32[32,768]{1,0:T(8,128)S(1)}, f32[32,768]{1,0:T(8,128)S(1)}, u32[]{:S(2)}, u32[]{:S(2)}) %collective-permute-start.2) | collective-permute-done | bytes 98336 | tf_op jit(solution)/shard_map/while/body/eval_jaxpr/ppermute | solution.py:12
  199.1 2.4 collective-permute-start
  206.5 4.7 %collective-permute-done.2 = f32[32,768]{1,0:T(8,128)S(1)} collective-permute-done((f32[32,768]{1,0:T(8,128)S(1)}, f32[32,768]{1,0:T(8,128)S(1)}, u32[]{:S(2)}, u32[]{:S(2)}) %collective-permute-start.2) | collective-permute-done | bytes 98336 | tf_op jit(solution)/shard_map/while/body/eval_jaxpr/ppermute | solution.py:12
  217.8 5.1 %collective-permute-done.2 = f32[32,768]{1,0:T(8,128)S(1)} collective-permute-done((f32[32,768]{1,0:T(8,128)S(1)}, f32[32,768]{1,0:T(8,128)S(1)}, u32[]{:S(2)}, u32[]{:S(2)}) %collective-permute-start.2) | collective-permute-done | bytes 98336 | tf_op jit(solution)/shard_map/while/body/eval_jaxpr/ppermute | solution.py:12
  229.5 6.0 %collective-permute-done.2 = f32[32,768]{1,0:T(8,128)S(1)} collective-permute-done((f32[32,768]{1,0:T(8,128)S(1)}, f32[32,768]{1,0:T(8,128)S(1)}, u32[]{:S(2)}, u32[]{:S(2)}) %collective-permute-start.2) | collective-permute-done | bytes 98336 | tf_op jit(solution)/shard_map/while/body/eval_jaxpr/ppermute | solution.py:12
  236.7 83.9 %reduce-scatter.2.cloned.1.call-done = f32[32,768]{1,0:T(8,128)} async-done(((f32[512,768]{1,0:T(8,128)}), f32[32,768]{1,0:T(8,128)}) %reduce-scatter.2.cloned.1.call-update) | async-done | bytes 98320 | tf_op jit(solution)/shard_map/reduce_scatter | solution.py:89
  (195 shorter events, 84.2 us)
Async XLA Ops:
  7.2 313.4 %reduce-scatter.2.cloned.1.call-start = ((), (), s32[]{:S(2)}) async-start(), calls=%async_computation.1 | async-start | bytes 1671168 | tf_op jit(solution)/shard_map/reduce_scatter | solution.py:89
  32.4 10.9 %collective-permute-start.1 = (f32[32]{0:T(128)S(1)}, f32[32]{0:T(128)S(1)}, u32[]{:S(2)}, u32[]{:S(2)}) collective-permute-start(f32[32]{0:T(128)S(1)} %copy.14), channel_id=1, source_target_pairs={{15,0},{0,1},{1,2},{2,3},{3,4},{4,5},{5,6},{6,7},{7,8},{8,9},{9,10... | collective-permute-start | bytes 392 | tf_op jit(solution)/shard_map/while/body/eval_jaxpr/ppermute | solution.py:12
  35.2 8.1 %collective-permute-start = (bf16[32,768]{1,0:T(8,128)(2,1)S(1)}, bf16[32,768]{1,0:T(8,128)(2,1)S(1)}, u32[]{:S(2)}, u32[]{:S(2)}) collective-permute-start(bf16[32,768]{1,0:T(8,128)(2,1)S(1)} %copy.13), channel_id=1, source_target_pairs={{15,0},{0,1},{1,2},{2,3},{3,4},{4,5},{5,6},{6,7},{7,8},{8,9},{9,10... | collective-permute-start | bytes 147464 | tf_op jit(solution)/shard_map/while/body/eval_jaxpr/ppermute | solution.py:12
  39.4 7.2 %collective-permute-start.2 = (f32[32,768]{1,0:T(8,128)S(1)}, f32[32,768]{1,0:T(8,128)S(1)}, u32[]{:S(2)}, u32[]{:S(2)}) collective-permute-start(f32[32,768]{1,0:T(8,128)S(1)} %fusion.22), channel_id=1, source_target_pairs={{15,0},{0,1},{1,2},{2,3},{3,4},{4,5},{5,6},{6,7},{7,8},{8,9},{9,10... | collective-permute-start | bytes 294920 | tf_op jit(solution)/shard_map/while/body/eval_jaxpr/ppermute | solution.py:12
  46.6 8.6 %collective-permute-start.1 = (f32[32]{0:T(128)S(1)}, f32[32]{0:T(128)S(1)}, u32[]{:S(2)}, u32[]{:S(2)}) collective-permute-start(f32[32]{0:T(128)S(1)} %copy.14), channel_id=1, source_target_pairs={{15,0},{0,1},{1,2},{2,3},{3,4},{4,5},{5,6},{6,7},{7,8},{8,9},{9,10... | collective-permute-start | bytes 392 | tf_op jit(solution)/shard_map/while/body/eval_jaxpr/ppermute | solution.py:12
  47.1 8.1 %collective-permute-start = (bf16[32,768]{1,0:T(8,128)(2,1)S(1)}, bf16[32,768]{1,0:T(8,128)(2,1)S(1)}, u32[]{:S(2)}, u32[]{:S(2)}) collective-permute-start(bf16[32,768]{1,0:T(8,128)(2,1)S(1)} %copy.13), channel_id=1, source_target_pairs={{15,0},{0,1},{1,2},{2,3},{3,4},{4,5},{5,6},{6,7},{7,8},{8,9},{9,10... | collective-permute-start | bytes 147464 | tf_op jit(solution)/shard_map/while/body/eval_jaxpr/ppermute | solution.py:12
  52.2 7.2 %collective-permute-start.2 = (f32[32,768]{1,0:T(8,128)S(1)}, f32[32,768]{1,0:T(8,128)S(1)}, u32[]{:S(2)}, u32[]{:S(2)}) collective-permute-start(f32[32,768]{1,0:T(8,128)S(1)} %fusion.22), channel_id=1, source_target_pairs={{15,0},{0,1},{1,2},{2,3},{3,4},{4,5},{5,6},{6,7},{7,8},{8,9},{9,10... | collective-permute-start | bytes 294920 | tf_op jit(solution)/shard_map/while/body/eval_jaxpr/ppermute | solution.py:12
  59.4 8.2 %collective-permute-start.1 = (f32[32]{0:T(128)S(1)}, f32[32]{0:T(128)S(1)}, u32[]{:S(2)}, u32[]{:S(2)}) collective-permute-start(f32[32]{0:T(128)S(1)} %copy.14), channel_id=1, source_target_pairs={{15,0},{0,1},{1,2},{2,3},{3,4},{4,5},{5,6},{6,7},{7,8},{8,9},{9,10... | collective-permute-start | bytes 392 | tf_op jit(solution)/shard_map/while/body/eval_jaxpr/ppermute | solution.py:12
  59.4 8.2 %collective-permute-start = (bf16[32,768]{1,0:T(8,128)(2,1)S(1)}, bf16[32,768]{1,0:T(8,128)(2,1)S(1)}, u32[]{:S(2)}, u32[]{:S(2)}) collective-permute-start(bf16[32,768]{1,0:T(8,128)(2,1)S(1)} %copy.13), channel_id=1, source_target_pairs={{15,0},{0,1},{1,2},{2,3},{3,4},{4,5},{5,6},{6,7},{7,8},{8,9},{9,10... | collective-permute-start | bytes 147464 | tf_op jit(solution)/shard_map/while/body/eval_jaxpr/ppermute | solution.py:12
  65.0 7.2 %collective-permute-start.2 = (f32[32,768]{1,0:T(8,128)S(1)}, f32[32,768]{1,0:T(8,128)S(1)}, u32[]{:S(2)}, u32[]{:S(2)}) collective-permute-start(f32[32,768]{1,0:T(8,128)S(1)} %fusion.22), channel_id=1, source_target_pairs={{15,0},{0,1},{1,2},{2,3},{3,4},{4,5},{5,6},{6,7},{7,8},{8,9},{9,10... | collective-permute-start | bytes 294920 | tf_op jit(solution)/shard_map/while/body/eval_jaxpr/ppermute | solution.py:12
  72.2 8.5 %collective-permute-start.1 = (f32[32]{0:T(128)S(1)}, f32[32]{0:T(128)S(1)}, u32[]{:S(2)}, u32[]{:S(2)}) collective-permute-start(f32[32]{0:T(128)S(1)} %copy.14), channel_id=1, source_target_pairs={{15,0},{0,1},{1,2},{2,3},{3,4},{4,5},{5,6},{6,7},{7,8},{8,9},{9,10... | collective-permute-start | bytes 392 | tf_op jit(solution)/shard_map/while/body/eval_jaxpr/ppermute | solution.py:12
  72.3 8.4 %collective-permute-start = (bf16[32,768]{1,0:T(8,128)(2,1)S(1)}, bf16[32,768]{1,0:T(8,128)(2,1)S(1)}, u32[]{:S(2)}, u32[]{:S(2)}) collective-permute-start(bf16[32,768]{1,0:T(8,128)(2,1)S(1)} %copy.13), channel_id=1, source_target_pairs={{15,0},{0,1},{1,2},{2,3},{3,4},{4,5},{5,6},{6,7},{7,8},{8,9},{9,10... | collective-permute-start | bytes 147464 | tf_op jit(solution)/shard_map/while/body/eval_jaxpr/ppermute | solution.py:12
  79.0 7.2 %collective-permute-start.2 = (f32[32,768]{1,0:T(8,128)S(1)}, f32[32,768]{1,0:T(8,128)S(1)}, u32[]{:S(2)}, u32[]{:S(2)}) collective-permute-start(f32[32,768]{1,0:T(8,128)S(1)} %fusion.22), channel_id=1, source_target_pairs={{15,0},{0,1},{1,2},{2,3},{3,4},{4,5},{5,6},{6,7},{7,8},{8,9},{9,10... | collective-permute-start | bytes 294920 | tf_op jit(solution)/shard_map/while/body/eval_jaxpr/ppermute | solution.py:12
  86.2 7.3 %collective-permute-start.1 = (f32[32]{0:T(128)S(1)}, f32[32]{0:T(128)S(1)}, u32[]{:S(2)}, u32[]{:S(2)}) collective-permute-start(f32[32]{0:T(128)S(1)} %copy.14), channel_id=1, source_target_pairs={{15,0},{0,1},{1,2},{2,3},{3,4},{4,5},{5,6},{6,7},{7,8},{8,9},{9,10... | collective-permute-start | bytes 392 | tf_op jit(solution)/shard_map/while/body/eval_jaxpr/ppermute | solution.py:12
  86.2 7.3 %collective-permute-start = (bf16[32,768]{1,0:T(8,128)(2,1)S(1)}, bf16[32,768]{1,0:T(8,128)(2,1)S(1)}, u32[]{:S(2)}, u32[]{:S(2)}) collective-permute-start(bf16[32,768]{1,0:T(8,128)(2,1)S(1)} %copy.13), channel_id=1, source_target_pairs={{15,0},{0,1},{1,2},{2,3},{3,4},{4,5},{5,6},{6,7},{7,8},{8,9},{9,10... | collective-permute-start | bytes 147464 | tf_op jit(solution)/shard_map/while/body/eval_jaxpr/ppermute | solution.py:12
  92.1 7.2 %collective-permute-start.2 = (f32[32,768]{1,0:T(8,128)S(1)}, f32[32,768]{1,0:T(8,128)S(1)}, u32[]{:S(2)}, u32[]{:S(2)}) collective-permute-start(f32[32,768]{1,0:T(8,128)S(1)} %fusion.22), channel_id=1, source_target_pairs={{15,0},{0,1},{1,2},{2,3},{3,4},{4,5},{5,6},{6,7},{7,8},{8,9},{9,10... | collective-permute-start | bytes 294920 | tf_op jit(solution)/shard_map/while/body/eval_jaxpr/ppermute | solution.py:12
  104.3 7.2 %collective-permute-start.2 = (f32[32,768]{1,0:T(8,128)S(1)}, f32[32,768]{1,0:T(8,128)S(1)}, u32[]{:S(2)}, u32[]{:S(2)}) collective-permute-start(f32[32,768]{1,0:T(8,128)S(1)} %fusion.22), channel_id=1, source_target_pairs={{15,0},{0,1},{1,2},{2,3},{3,4},{4,5},{5,6},{6,7},{7,8},{8,9},{9,10... | collective-permute-start | bytes 294920 | tf_op jit(solution)/shard_map/while/body/eval_jaxpr/ppermute | solution.py:12
  116.2 7.2 %collective-permute-start.2 = (f32[32,768]{1,0:T(8,128)S(1)}, f32[32,768]{1,0:T(8,128)S(1)}, u32[]{:S(2)}, u32[]{:S(2)}) collective-permute-start(f32[32,768]{1,0:T(8,128)S(1)} %fusion.22), channel_id=1, source_target_pairs={{15,0},{0,1},{1,2},{2,3},{3,4},{4,5},{5,6},{6,7},{7,8},{8,9},{9,10... | collective-permute-start | bytes 294920 | tf_op jit(solution)/shard_map/while/body/eval_jaxpr/ppermute | solution.py:12
  127.5 8.2 %collective-permute-start.2 = (f32[32,768]{1,0:T(8,128)S(1)}, f32[32,768]{1,0:T(8,128)S(1)}, u32[]{:S(2)}, u32[]{:S(2)}) collective-permute-start(f32[32,768]{1,0:T(8,128)S(1)} %fusion.22), channel_id=1, source_target_pairs={{15,0},{0,1},{1,2},{2,3},{3,4},{4,5},{5,6},{6,7},{7,8},{8,9},{9,10... | collective-permute-start | bytes 294920 | tf_op jit(solution)/shard_map/while/body/eval_jaxpr/ppermute | solution.py:12
  139.4 7.2 %collective-permute-start.2 = (f32[32,768]{1,0:T(8,128)S(1)}, f32[32,768]{1,0:T(8,128)S(1)}, u32[]{:S(2)}, u32[]{:S(2)}) collective-permute-start(f32[32,768]{1,0:T(8,128)S(1)} %fusion.22), channel_id=1, source_target_pairs={{15,0},{0,1},{1,2},{2,3},{3,4},{4,5},{5,6},{6,7},{7,8},{8,9},{9,10... | collective-permute-start | bytes 294920 | tf_op jit(solution)/shard_map/while/body/eval_jaxpr/ppermute | solution.py:12
  146.6 7.2 %collective-permute-start.1 = (f32[32]{0:T(128)S(1)}, f32[32]{0:T(128)S(1)}, u32[]{:S(2)}, u32[]{:S(2)}) collective-permute-start(f32[32]{0:T(128)S(1)} %copy.14), channel_id=1, source_target_pairs={{15,0},{0,1},{1,2},{2,3},{3,4},{4,5},{5,6},{6,7},{7,8},{8,9},{9,10... | collective-permute-start | bytes 392 | tf_op jit(solution)/shard_map/while/body/eval_jaxpr/ppermute | solution.py:12
  146.6 7.2 %collective-permute-start = (bf16[32,768]{1,0:T(8,128)(2,1)S(1)}, bf16[32,768]{1,0:T(8,128)(2,1)S(1)}, u32[]{:S(2)}, u32[]{:S(2)}) collective-permute-start(bf16[32,768]{1,0:T(8,128)(2,1)S(1)} %copy.13), channel_id=1, source_target_pairs={{15,0},{0,1},{1,2},{2,3},{3,4},{4,5},{5,6},{6,7},{7,8},{8,9},{9,10... | collective-permute-start | bytes 147464 | tf_op jit(solution)/shard_map/while/body/eval_jaxpr/ppermute | solution.py:12
  158.8 8.2 %collective-permute-start.1 = (f32[32]{0:T(128)S(1)}, f32[32]{0:T(128)S(1)}, u32[]{:S(2)}, u32[]{:S(2)}) collective-permute-start(f32[32]{0:T(128)S(1)} %copy.14), channel_id=1, source_target_pairs={{15,0},{0,1},{1,2},{2,3},{3,4},{4,5},{5,6},{6,7},{7,8},{8,9},{9,10... | collective-permute-start | bytes 392 | tf_op jit(solution)/shard_map/while/body/eval_jaxpr/ppermute | solution.py:12
  158.8 8.1 %collective-permute-start = (bf16[32,768]{1,0:T(8,128)(2,1)S(1)}, bf16[32,768]{1,0:T(8,128)(2,1)S(1)}, u32[]{:S(2)}, u32[]{:S(2)}) collective-permute-start(bf16[32,768]{1,0:T(8,128)(2,1)S(1)} %copy.13), channel_id=1, source_target_pairs={{15,0},{0,1},{1,2},{2,3},{3,4},{4,5},{5,6},{6,7},{7,8},{8,9},{9,10... | collective-permute-start | bytes 147464 | tf_op jit(solution)/shard_map/while/body/eval_jaxpr/ppermute | solution.py:12
  172.7 7.8 %collective-permute-start.1 = (f32[32]{0:T(128)S(1)}, f32[32]{0:T(128)S(1)}, u32[]{:S(2)}, u32[]{:S(2)}) collective-permute-start(f32[32]{0:T(128)S(1)} %copy.14), channel_id=1, source_target_pairs={{15,0},{0,1},{1,2},{2,3},{3,4},{4,5},{5,6},{6,7},{7,8},{8,9},{9,10... | collective-permute-start | bytes 392 | tf_op jit(solution)/shard_map/while/body/eval_jaxpr/ppermute | solution.py:12
  172.7 7.8 %collective-permute-start = (bf16[32,768]{1,0:T(8,128)(2,1)S(1)}, bf16[32,768]{1,0:T(8,128)(2,1)S(1)}, u32[]{:S(2)}, u32[]{:S(2)}) collective-permute-start(bf16[32,768]{1,0:T(8,128)(2,1)S(1)} %copy.13), channel_id=1, source_target_pairs={{15,0},{0,1},{1,2},{2,3},{3,4},{4,5},{5,6},{6,7},{7,8},{8,9},{9,10... | collective-permute-start | bytes 147464 | tf_op jit(solution)/shard_map/while/body/eval_jaxpr/ppermute | solution.py:12
  185.7 7.6 %collective-permute-start.1 = (f32[32]{0:T(128)S(1)}, f32[32]{0:T(128)S(1)}, u32[]{:S(2)}, u32[]{:S(2)}) collective-permute-start(f32[32]{0:T(128)S(1)} %copy.14), channel_id=1, source_target_pairs={{15,0},{0,1},{1,2},{2,3},{3,4},{4,5},{5,6},{6,7},{7,8},{8,9},{9,10... | collective-permute-start | bytes 392 | tf_op jit(solution)/shard_map/while/body/eval_jaxpr/ppermute | solution.py:12
  185.7 7.6 %collective-permute-start = (bf16[32,768]{1,0:T(8,128)(2,1)S(1)}, bf16[32,768]{1,0:T(8,128)(2,1)S(1)}, u32[]{:S(2)}, u32[]{:S(2)}) collective-permute-start(bf16[32,768]{1,0:T(8,128)(2,1)S(1)} %copy.13), channel_id=1, source_target_pairs={{15,0},{0,1},{1,2},{2,3},{3,4},{4,5},{5,6},{6,7},{7,8},{8,9},{9,10... | collective-permute-start | bytes 147464 | tf_op jit(solution)/shard_map/while/body/eval_jaxpr/ppermute | solution.py:12
  191.9 7.2 %collective-permute-start.2 = (f32[32,768]{1,0:T(8,128)S(1)}, f32[32,768]{1,0:T(8,128)S(1)}, u32[]{:S(2)}, u32[]{:S(2)}) collective-permute-start(f32[32,768]{1,0:T(8,128)S(1)} %fusion.22), channel_id=1, source_target_pairs={{15,0},{0,1},{1,2},{2,3},{3,4},{4,5},{5,6},{6,7},{7,8},{8,9},{9,10... | collective-permute-start | bytes 294920 | tf_op jit(solution)/shard_map/while/body/eval_jaxpr/ppermute | solution.py:12
  199.1 7.4 %collective-permute-start = (bf16[32,768]{1,0:T(8,128)(2,1)S(1)}, bf16[32,768]{1,0:T(8,128)(2,1)S(1)}, u32[]{:S(2)}, u32[]{:S(2)}) collective-permute-start(bf16[32,768]{1,0:T(8,128)(2,1)S(1)} %copy.13), channel_id=1, source_target_pairs={{15,0},{0,1},{1,2},{2,3},{3,4},{4,5},{5,6},{6,7},{7,8},{8,9},{9,10... | collective-permute-start | bytes 147464 | tf_op jit(solution)/shard_map/while/body/eval_jaxpr/ppermute | solution.py:12
  204.0 7.2 %collective-permute-start.2 = (f32[32,768]{1,0:T(8,128)S(1)}, f32[32,768]{1,0:T(8,128)S(1)}, u32[]{:S(2)}, u32[]{:S(2)}) collective-permute-start(f32[32,768]{1,0:T(8,128)S(1)} %fusion.22), channel_id=1, source_target_pairs={{15,0},{0,1},{1,2},{2,3},{3,4},{4,5},{5,6},{6,7},{7,8},{8,9},{9,10... | collective-permute-start | bytes 294920 | tf_op jit(solution)/shard_map/while/body/eval_jaxpr/ppermute | solution.py:12
  227.2 8.3 %collective-permute-start.2 = (f32[32,768]{1,0:T(8,128)S(1)}, f32[32,768]{1,0:T(8,128)S(1)}, u32[]{:S(2)}, u32[]{:S(2)}) collective-permute-start(f32[32,768]{1,0:T(8,128)S(1)} %fusion.22), channel_id=1, source_target_pairs={{15,0},{0,1},{1,2},{2,3},{3,4},{4,5},{5,6},{6,7},{7,8},{8,9},{9,10... | collective-permute-start | bytes 294920 | tf_op jit(solution)/shard_map/while/body/eval_jaxpr/ppermute | solution.py:12
  (22 other events, 187.0 us)
Sparse Core Ops, SparseCore 0:
  236.8 83.7 reduce-scatter.1
where the time goes:
time: 331 us; the launch traced here: 328 us
  waiting for transfers between devices  172 us (52%)
  matrix products  58.7 us (18%)
  starting transfers between devices  55.9 us (17%)
  blocking collectives  23.4 us (7%)
  between operations  14.8 us (4%)
    ppermute x48, waiting for transfers between devices, passed_along(): return lax.ppermute(block, axis, route)  87.6 us
    reduce_scatter x1, waiting for transfers between devices, local(): lax.psum_scatter(block_total, 'slab', scatter_dimension=0, tiled=True)  83.9 us
    ppermute x48, starting transfers between devices, passed_along(): return lax.ppermute(block, axis, route)  55.8 us
    dot_general x16, matrix products, tile_gradients(): lax.dot_general(query_rows, passage_block, (((1,), (1,)), ((), ())), pref...  23.9 us
    all_gather x1, blocking collectives, local(): passage_block = lax.all_gather(passages, 'slab', axis=0, tiled=True)  23.4 us
    dot_general x16, matrix products, tile_gradients(): lax.dot_general(weights, rows_wide, (((0,), (0,)), ((), ())), precision=l...  19 us
    dot_general x16, matrix products, tile_gradients(): jnp.dot(weights, block_wide, precision=lax.Precision.HIGHEST, preferred_e...  15.9 us
  transfers between devices with their start and end apart: 49, of which 28 were waited for; matrix products, arithmetic and copies ran while one was open for 18% of the time, Pallas kernels for 0%

commit v1 on v0

v1 whole, which is shorter than its diff:
```python
import math

import jax
import jax.numpy as jnp
from jax import lax
from jax.experimental import pallas as pl
from jax.experimental.pallas import tpu as pltpu
from jax.sharding import PartitionSpec as P

MESH = pl.DeviceIdType.MESH
F32, BF16 = jnp.float32, jnp.bfloat16
ROWS = 32
HALF = 16
BATCH = 8192
LOG2E = math.log2(math.e)
TOP = math.log(BATCH) + 3.5
BOUND = 512 * 6.0 * 2.0**-30
TINY = 1e-37


def encode(value, inverse):
    t = value * inverse
    u = t * jnp.abs(t)
    return (u * jnp.abs(u)).astype(BF16)


def decode(coded, scale):
    wide = coded.astype(F32)
    r = lax.rsqrt(jnp.maximum(jnp.abs(wide), TINY))
    return (wide * r) * (r * lax.rsqrt(r)) * scale


def body(
    width,
    q_in, p_in, qn_in, pn_in, loss_ref,
    oq_ref, op_ref,
    q_all, p_all, qn_all, pn_all,
    w_hi, w_lo, g_q, g_p, xq_out, xq_in,
    zs1, zs2, zd_in, zf_in, zh_in, z2_in,
    pa_out, pa_in, pb_out, pb_in,
    fa_out, fa_in, fb_out, fb_in,
    sc_me, sc_q, sc_qr, sc_pa, sc_pb, sx_in, sz_in, sz2_in, sy1_in, sx1_in, sfa_in, sfb_in,
    ssem, lsem, q_sem, qh_sem, qn_sem, pa_sem, pb_sem, pn_sem,
    xq_sem, xs_sem, zd_sem, zf_sem, zh_sem, z2_sem, zsc_sem, zsc2_sem,
    ra_sem, rb_sem, ras_sem, rbs_sem, fa_sem, fb_sem, fas_sem, fbs_sem,
):
    slab, blk = lax.axis_index("slab"), lax.axis_index("blk")
    x, yl, c = slab // 4, (slab // 2) % 2, slab % 2
    z, yh = blk // 2, blk % 2
    y = yh * 2 + yl
    other = 1 - c
    same = c == yh

    def dev(xx, yy, zz, cc):
        return (xx * 4 + (yy % 2) * 2 + cc, zz * 2 + yy // 2)

    def up(value, by, size):
        return (value + by) % size

    pending = []
    count = [0]

    def send(build, when=None):
        index = count[0]
        count[0] += 1

        def make():
            src, dst, rsem, to = build()
            return pltpu.make_async_remote_copy(
                src_ref=src, dst_ref=dst, send_sem=ssem.at[index], recv_sem=rsem, device_id=to, device_id_type=MESH
            )

        if when is None:
            make().start()
        else:
            pl.when(when)(lambda: make().start())
        pending.append((make, when))

    def wait(dst, rsem):
        pltpu.make_async_remote_copy(
            src_ref=dst, dst_ref=dst, send_sem=lsem.at[0], recv_sem=rsem, device_id=dev(x, y, z, other), device_id_type=MESH
        ).wait_recv()

    barrier = pltpu.get_barrier_semaphore()
    peers = [dev(x, y, z, other)]
    peers += [dev(x, y, up(z, d, 8), c) for d in (1, 2, 6, 7)]
    peers += [dev(up(x, d, 4), y, z, cc) for d in (1, 2, 3) for cc in (0, 1)]
    peers += [dev(x, up(y, d, 4), z, cc) for d in (1, 2, 3) for cc in (0, 1)]
    for peer in peers:
        pl.semaphore_signal(barrier, inc=1, device_id=peer, device_id_type=MESH)

    me_q = c * 8 + z
    local_q = pltpu.make_async_copy(q_in, q_all.at[me_q], lsem.at[1])
    local_q.start()
    qn_all[me_q, :, :ROWS] = qn_in[...].reshape(1, ROWS)
    low, high = pl.ds(0, HALF), pl.ds(HALF, HALF)

    def local_p(half, sem):
        return pltpu.make_async_copy(p_in.at[half], p_all.at[slab, half], sem.at[slab])

    def local_pn():
        return pltpu.make_async_copy(pn_in, pn_all.at[0], pn_sem.at[0])

    @pl.when(same)
    def _():
        local_p(low, pa_sem).start()
        local_p(high, pb_sem).start()
        local_pn().start()

    pl.semaphore_wait(barrier, len(peers))

    for d in (2, 1, 3):
        send(lambda d=d: (p_in.at[low], p_all.at[slab, low], pa_sem.at[slab], dev(up(x, d, 4), y, z, yh)))
        send(lambda d=d: (p_in.at[high], p_all.at[slab, high], pb_sem.at[slab], dev(x, up(y, d, 4), z, yh)))
    for d in (2, 6, 1, 7):
        send(lambda d=d: (q_in, q_all.at[me_q], q_sem.at[me_q], dev(x, y, up(z, d, 8), c)))
        send(lambda d=d: (qn_all.at[me_q], qn_all.at[me_q], qn_sem.at[me_q], dev(x, y, up(z, d, 8), c)))
    send(lambda: (p_in.at[low], p_all.at[slab, low], pa_sem.at[slab], dev(x, y, z, other)), jnp.logical_not(same))
    send(lambda: (p_in.at[high], p_all.at[slab, high], pb_sem.at[slab], dev(x, y, z, other)), jnp.logical_not(same))
    send(lambda: (pn_in, pn_all.at[0], pn_sem.at[0], dev(x, up(y, 2, 4), z, c)), same)

    def q_send(slot, to, half=None, sem=None, norm=True):
        if half is None:
            send(lambda: (q_all.at[slot], q_all.at[slot], q_sem.at[slot], to))
        else:
            send(lambda: (q_all.at[slot, half], q_all.at[slot, half], sem, to))
        if norm:
            row = lambda: qn_all.at[slot]
            send(lambda: (row(), row(), qn_sem.at[slot], to))

    def q_wait(slot, norm=True):
        wait(q_all.at[slot], q_sem.at[slot])
        if norm:
            wait(qn_all.at[slot], qn_sem.at[slot])

    partner = dev(x, y, z, other)
    send(lambda: (q_in, q_all.at[me_q], q_sem.at[me_q], partner))
    send(lambda: (qn_all.at[me_q], qn_all.at[me_q], qn_sem.at[me_q], partner))

    for d, near, far, half, hsem in ((6, 1, 2, low, 0), (2, 7, 6, high, 1)):
        slot = c * 8 + up(z, d, 8)
        q_wait(slot)
        q_send(slot, dev(x, y, up(z, far, 8), c), half, qh_sem.at[hsem], norm=hsem == 0)
        q_send(slot, dev(x, y, up(z, near, 8), c))
        q_send(slot, partner)
    for d in (1, 7):
        slot = c * 8 + up(z, d, 8)
        q_wait(slot)
        q_send(slot, partner)

    for e in (0, 1, 3, 2):
        for cc in (0, 1):
            slot = up(x, e, 4) * 4 + yl * 2 + cc
            pl.when(same)(lambda slot=slot: wait(p_all.at[slot, low], pa_sem.at[slot]))
            for d in (2, 1, 3):
                send(
                    lambda slot=slot, d=d: (
                        p_all.at[slot, low], p_all.at[slot, low], pa_sem.at[slot], dev(x, up(y, d, 4), z, c)
                    ),
                    same,
                )
    for e in range(2):
        for cc in (0, 1):
            slot = x * 4 + e * 2 + cc
            wait(p_all.at[slot, high], pb_sem.at[slot])
            for d in (2, 1, 3):
                send(
                    lambda slot=slot, d=d: (
                        p_all.at[slot, high], p_all.at[slot, high], pb_sem.at[slot], dev(up(x, d, 4), y, z, c)
                    )
                )

    for d in (3, 5):
        slot = c * 8 + up(z, d, 8)
        q_wait(slot)
        q_send(slot, partner)
    slot = c * 8 + up(z, 4, 8)
    wait(q_all.at[slot, low], qh_sem.at[0])
    wait(q_all.at[slot, high], qh_sem.at[1])
    wait(qn_all.at[slot], qn_sem.at[slot])
    q_send(slot, partner)

    for e in range(4):
        for yy in (0, 1):
            for cc in (0, 1):
                slot = up(x, e, 4) * 4 + yy * 2 + cc
                pl.when(jnp.logical_not(jnp.logical_and(same, yl == yy)))(
                    lambda slot=slot: wait(p_all.at[slot, low], pa_sem.at[slot])
                )
                if e:
                    wait(p_all.at[slot, high], pb_sem.at[slot])
    for d in range(8):
        q_wait(other * 8 + up(z, d, 8))
    local_q.wait()
    wait(pn_all.at[0], pn_sem.at[0])

    scale = 2.0 / math.sqrt(width)
    g = (0.5 * scale) * loss_ref[0]
    columns = pn_all.shape[1]
    b = g * jnp.exp(TOP - pn_all[...])
    a_t = (g * jnp.exp(TOP - qn_all[...].reshape(16, 128))).T
    passages = p_all[...].reshape(columns, width)
    largest = jnp.zeros((8, 128), F32)
    column = lax.broadcasted_iota(jnp.int32, (ROWS, columns), 1) - lax.broadcasted_iota(jnp.int32, (ROWS, columns), 0)
    for chunk in range(4):
        rows = q_all[pl.ds(chunk * 4, 4)].reshape(4 * ROWS, width)
        scores = lax.dot_general(rows, passages, (((1,), (1,)), ((), ())), preferred_element_type=F32)
        terms = jnp.exp2(scores * (scale * LOG2E) - TOP * LOG2E)
        for k in range(4):
            slot = chunk * 4 + k
            first = ((x * 4 + yl * 2 + slot // 8) * 16 + (slot % 8) * 2 + yh) * ROWS - (z * 2 + c) * columns
            here = slice(k * ROWS, (k + 1) * ROWS)
            weights = terms[here] * (a_t[:ROWS, slot : slot + 1] + b) - jnp.where(column == first, 2.0 * g, 0.0)
            top = weights.astype(BF16)
            at = pl.ds(slot * ROWS, ROWS)
            w_hi[at, :] = top
            w_lo[at, :] = (weights - top.astype(F32)).astype(BF16)
            size = jnp.abs(weights)
            size = jnp.maximum(size[:HALF], size[HALF:])
            size = jnp.maximum(size[:8], size[8:])
            for j in range(columns // 128):
                largest = jnp.maximum(largest, size[:, j * 128 : (j + 1) * 128])
    mine = jnp.maximum(jnp.max(largest, axis=(0, 1), keepdims=True), 1e-30) * BOUND
    mine = jnp.broadcast_to(mine, (1, 128))
    sc_me[0] = mine
    send(lambda: (sc_me.at[0], sx_in.at[0], xs_sem.at[0], partner))
    for d in (2, 1, 3):
        send(lambda d=d: (sc_me.at[0], sx1_in.at[3 - d], rbs_sem.at[3 - d], dev(up(x, d, 4), y, z, c)))
    for yy in (0, 1):
        to = 2 * c + yy
        back = (y - to + 3) % 4
        send(
            lambda to=to, back=back: (sc_me.at[0], sy1_in.at[back], ras_sem.at[back], dev(x, to, z, c)),
            to != y,
        )

    def lane(row):
        return row[:, :1]

    inverse = lane(1.0 / mine)

    for chunk in range(2):
        at = pl.ds(pl.multiple_of(other * 8 * ROWS + chunk * 4 * ROWS, 4 * ROWS), 4 * ROWS)
        part = jnp.dot(w_hi[at, :], passages, preferred_element_type=F32)
        part += jnp.dot(w_lo[at, :], passages, preferred_element_type=F32)
        to = pl.ds(chunk * 4, 4)
        xq_out[to] = part.reshape(4, ROWS, width)
        send(lambda to=to, chunk=chunk: (xq_out.at[to], xq_in.at[to], xq_sem.at[chunk], partner))
    for chunk in range(2):
        at = pl.ds(pl.multiple_of(c * 8 * ROWS + chunk * 4 * ROWS, 4 * ROWS), 4 * ROWS)
        part = jnp.dot(w_hi[at, :], passages, preferred_element_type=F32)
        part += jnp.dot(w_lo[at, :], passages, preferred_element_type=F32)
        g_q[pl.ds(chunk * 4, 4)] = part.reshape(4, ROWS, width)

    queries = q_all[...].reshape(16 * ROWS, width)
    across = (((0,), (0,)), ((), ()))

    def passage_chunk(d):
        xm = up(x, d, 4)
        at = pl.ds(pl.multiple_of(xm * 4 * ROWS, 4 * ROWS), 4 * ROWS)
        part = lax.dot_general(w_hi[:, at], queries, across, preferred_element_type=F32)
        part += lax.dot_general(w_lo[:, at], queries, across, preferred_element_type=F32)
        part = part.reshape(2, 2, ROWS, width)
        g_p[xm] = part
        coded = encode(part, inverse)
        if d:
            pb_out[3 - d] = coded[:, :, HALF:]
            send(
                lambda: (pb_out.at[3 - d], pb_in.at[3 - d], rb_sem.at[3 - d], dev(xm, y, z, c)),
            )
        for yy in (0, 1):
            to = 2 * c + yy
            back = (y - to + 3) % 4
            pa_out[yy, xm] = coded[yy, :, :HALF]
            send(
                lambda yy=yy, to=to, back=back: (
                    pa_out.at[yy, xm], pa_in.at[back, xm], ra_sem.at[back, xm], dev(x, to, z, c)
                ),
                to != y,
            )

    passage_chunk(2)

    wait(sx_in.at[0], xs_sem.at[0])
    both = mine + sx_in[0]
    sc_q[0] = both
    for chunk in range(2):
        wait(xq_in.at[pl.ds(chunk * 4, 4)], xq_sem.at[chunk])
    for d in (1, 2, 6, 7):
        send(lambda d=d: (sc_q.at[0], sz_in.at[8 - d], zsc_sem.at[8 - d], dev(x, y, up(z, d, 8), c)))
    inverse_q = lane(1.0 / both)

    def column_sum(zz):
        return g_q[zz] + xq_in[zz]

    far = encode(column_sum(up(z, 4, 8)), inverse_q)
    zs1[4, low] = far[:HALF]
    zs1[4, high] = far[HALF:]
    for i, d in enumerate((5, 3)):
        zs1[i] = encode(column_sum(up(z, d, 8)), inverse_q)
    for i, d in enumerate((1, 7)):
        zs1[2 + i] = encode(column_sum(up(z, d, 8)), inverse_q)
    send(lambda: (zs1.at[4, low], zh_in.at[0], zh_sem.at[0], dev(x, y, up(z, 6, 8), c)))
    send(lambda: (zs1.at[4, high], zh_in.at[1], zh_sem.at[1], dev(x, y, up(z, 2, 8), c)))
    send(lambda: (zs1.at[0], zf_in.at[0], zf_sem.at[0], dev(x, y, up(z, 7, 8), c)))
    send(lambda: (zs1.at[1], zf_in.at[1], zf_sem.at[1], dev(x, y, up(z, 1, 8), c)))
    send(lambda: (zs1.at[2], zd_in.at[0], zd_sem.at[0], dev(x, y, up(z, 1, 8), c)))
    send(lambda: (zs1.at[3], zd_in.at[1], zd_sem.at[1], dev(x, y, up(z, 7, 8), c)))

    for d in (1, 3, 0):
        passage_chunk(d)

    for d in (1, 2, 6, 7):
        wait(sz_in.at[d], zsc_sem.at[d])
    for i in (0, 1):
        near, far_ = (1, 2) if i == 0 else (7, 6)
        wait(zf_in.at[i], zf_sem.at[i])
        wait(zh_in.at[i], zh_sem.at[i])
        total = both + sz_in[near] + sz_in[far_]
        sc_qr[i] = total
        value = column_sum(up(z, 6 if i == 0 else 2, 8)) + decode(zf_in[i], lane(sz_in[near]))
        extra = decode(zh_in[i], lane(sz_in[far_]))
        inv = lane(1.0 / total)
        first_half, second_half = value[:HALF], value[HALF:]
        if i == 0:
            first_half = first_half + extra
        else:
            second_half = second_half + extra
        zs2[i, low] = encode(first_half, inv)
        zs2[i, high] = encode(second_half, inv)
    for i in (0, 1):
        to = dev(x, y, up(z, 6 if i == 0 else 2, 8), c)
        send(lambda i=i, to=to: (sc_qr.at[i], sz2_in.at[i], zsc2_sem.at[i], to))
        send(lambda i=i, to=to: (zs2.at[i], z2_in.at[i], z2_sem.at[i], to))

    for d in (1, 2, 3):
        wait(sx1_in.at[d - 1], rbs_sem.at[d - 1])
        wait(pb_in.at[d - 1], rb_sem.at[d - 1])
    total_b = mine + sx1_in[0] + sx1_in[1] + sx1_in[2]
    sc_pb[0] = total_b
    inv_b = lane(1.0 / total_b)
    for yy in (0, 1):
        for cc in (0, 1):
            value = g_p[x, yy, cc, HALF:]
            for d in (1, 2, 3):
                value = value + decode(pb_in[d - 1, yy, cc], lane(sx1_in[d - 1]))
            fb_out[yy, cc] = encode(value, inv_b)
    for yy in (0, 1):
        for cc in (0, 1):
            to = 2 * c + yy
            back = (y - to + 4) % 4
            mine_too = jnp.logical_and(to == y, c == cc)

            @pl.when(mine_too)
            def _(yy=yy, cc=cc):
                fb_in[0] = fb_out[yy, cc]
                sfb_in[0] = total_b

            away = jnp.logical_not(mine_too)
            send(
                lambda to=to, back=back, cc=cc: (sc_pb.at[0], sfb_in.at[back], fbs_sem.at[back], dev(x, to, z, cc)), away
            )
            send(
                lambda to=to, back=back, yy=yy, cc=cc: (
                    fb_out.at[yy, cc], fb_in.at[back], fb_sem.at[back], dev(x, to, z, cc)
                ),
                away,
            )

    @pl.when(same)
    def _():
        for d in (1, 2, 3):
            wait(sy1_in.at[d - 1], ras_sem.at[d - 1])
        total_a = mine + sy1_in[0] + sy1_in[1] + sy1_in[2]
        sc_pa[0] = total_a
        inv_a = lane(1.0 / total_a)
        for e in (2, 1, 3, 0):
            xm = up(x, e, 4)
            for d in (1, 2, 3):
                wait(pa_in.at[d - 1, xm], ra_sem.at[d - 1, xm])
            for cc in (0, 1):
                value = g_p[xm, yl, cc, :HALF]
                for d in (1, 2, 3):
                    value = value + decode(pa_in[d - 1, xm, cc], lane(sy1_in[d - 1]))
                fa_out[e, cc] = encode(value, inv_a)
        fa_in[0] = fa_out[0, c]
        sfa_in[0] = total_a

    for e in (2, 1, 3):
        for cc in (0, 1):
            back = 4 - e
            send(
                lambda e=e, cc=cc, back=back: (sc_pa.at[0], sfa_in.at[back], fas_sem.at[back], dev(up(x, e, 4), y, z, cc)),
                same,
            )
            send(
                lambda e=e, cc=cc, back=back: (
                    fa_out.at[e, cc], fa_in.at[back], fa_sem.at[back], dev(up(x, e, 4), y, z, cc)
                ),
                same,
            )
    send(lambda: (sc_pa.at[0], sfa_in.at[0], fas_sem.at[0], partner), same)
    send(lambda: (fa_out.at[0, other], fa_in.at[0], fa_sem.at[0], partner), same)

    value = column_sum(z)
    for i, d in ((0, 7), (1, 1)):
        wait(zd_in.at[i], zd_sem.at[i])
        value = value + decode(zd_in[i], lane(sz_in[d]))
    for i in (0, 1):
        wait(sz2_in.at[i], zsc2_sem.at[i])
        wait(z2_in.at[i], z2_sem.at[i])
        value = value + decode(z2_in[i], lane(sz2_in[i]))
    oq_ref[...] = value

    for parts, scales, psem, sem, half in ((fb_in, sfb_in, fb_sem, fbs_sem, high), (fa_in, sfa_in, fa_sem, fas_sem, low)):
        for e in range(4):

            def arrived(e=e, parts=parts, scales=scales, psem=psem, sem=sem):
                wait(scales.at[e], sem.at[e])
                wait(parts.at[e], psem.at[e])

            if e:
                arrived()
            else:
                pl.when(jnp.logical_not(same))(arrived)
        value = decode(parts[0], lane(scales[0]))
        for e in (1, 2, 3):
            value = value + decode(parts[e], lane(scales[e]))
        op_ref[half, :] = value

    for make, when in pending:
        if when is None:
            make().wait_send()
        else:
            pl.when(when)(lambda make=make: make().wait_send())


N_SENDS = 200


def local(queries, passages, query_lognorm, passage_lognorm, loss_cotangent):
    width = queries.shape[1]
    columns = passage_lognorm.shape[0]
    dma = pltpu.SemaphoreType.DMA
    vm = pltpu.VMEM
    scratch = [
        vm((16, ROWS, width), BF16), vm((16, ROWS, width), BF16), vm((16, 1, 128), F32), vm((1, columns), F32),
        vm((16 * ROWS, columns), BF16), vm((16 * ROWS, columns), BF16),
        vm((8, ROWS, width), F32), vm((4, 2, 2, ROWS, width), F32),
        vm((8, ROWS, width), F32), vm((8, ROWS, width), F32),
        vm((5, ROWS, width), BF16), vm((2, ROWS, width), BF16), vm((2, ROWS, width), BF16),
        vm((2, ROWS, width), BF16), vm((2, HALF, width), BF16), vm((2, ROWS, width), BF16),
        vm((2, 4, 2, HALF, width), BF16), vm((3, 4, 2, HALF, width), BF16),
        vm((3, 2, 2, HALF, width), BF16), vm((3, 2, 2, HALF, width), BF16),
        vm((4, 2, HALF, width), BF16), vm((4, HALF, width), BF16),
        vm((2, 2, HALF, width), BF16), vm((4, HALF, width), BF16),
        *[vm((n, 1, 128), F32) for n in (1, 1, 2, 1, 1, 1, 8, 2, 3, 3, 4, 4)],
        dma((N_SENDS,)), dma((2,)), dma((16,)), dma((2,)), dma((16,)), dma((16,)), dma((16,)), dma((1,)),
        dma((2,)), dma((1,)), dma((2,)), dma((2,)), dma((2,)), dma((2,)), dma((8,)), dma((2,)),
        dma((3, 4)), dma((3,)), dma((3,)), dma((3,)), dma((4,)), dma((4,)), dma((4,)), dma((4,)),
    ]
    anywhere = pl.BlockSpec(memory_space=pl.ANY)
    out = jax.ShapeDtypeStruct(queries.shape, F32)

    def kernel(*refs):
        body(width, *refs)

    return pl.pallas_call(
        kernel,
        out_shape=(out, out),
        in_specs=[anywhere, anywhere, pl.BlockSpec(memory_space=pltpu.VMEM), anywhere] + [pl.BlockSpec(memory_space=pltpu.SMEM)],
        out_specs=[pl.BlockSpec(memory_space=pltpu.VMEM)] * 2,
        scratch_shapes=scratch,
        compiler_params=pltpu.CompilerParams(collective_id=0, has_side_effects=True),
    )(queries, passages, query_lognorm, passage_lognorm, loss_cotangent.reshape(1))


def solution(mesh):
    return jax.shard_map(
        local,
        mesh=mesh,
        in_specs=(
            P(("slab", "blk"), None),
            P(("blk", "slab"), None),
            P(("slab", "blk")),
            P("blk"),
            P(),
        ),
        out_specs=(P(("slab", "blk"), None), P(("blk", "slab"), None)),
        check_vma=False,
    )
```

time: 331 us -> 46.3 us (0.14)
  waiting for transfers between devices: 172 us -> 0 us
  matrix products: 58.7 us -> 0 us
  starting transfers between devices: 55.9 us -> 0 us
  Pallas kernels: 0 us -> 42.6 us
  blocking collectives: 23.4 us -> 0 us
  between operations: 14.8 us -> 1.29 us
    ppermute x48 -> x0, waiting for transfers between devices: 87.6 us -> none  [passed_along(): return lax.ppermute(block, axis, route)]
    reduce_scatter x1 -> x0, waiting for transfers between devices: 83.9 us -> none  [local(): lax.psum_scatter(block_total, 'slab', scatter_dimension=0, tiled=True)]
    dot_general x48 -> x0, matrix products: 58.7 us -> none  [the longest x16 23.9 us: tile_gradients(): lax.dot_general(query_rows, passage_block, (((1,), (1,)), ((), ())), pref...]
    ppermute x48 -> x0, starting transfers between devices: 55.8 us -> none  [passed_along(): return lax.ppermute(block, axis, route)]
    pallas_call x0 -> x1, Pallas kernels: none -> 42.6 us  [local(): pl.pallas_call(kernel, out_shape=(out, out), in_specs=[anywhere, anywhere...]
    all_gather x1 -> x0, blocking collectives: 23.4 us -> none  [local(): passage_block = lax.all_gather(passages, 'slab', axis=0, tiled=True)]
  transfers between devices with their start and end apart: 49 -> 0, of which waited for: 28 -> 0; matrix products, arithmetic and copies ran while one was open for 18% -> 0% of each run, Pallas kernels for 0% -> 0%
where the time goes in v1:
time: 46.3 us; the launch traced here: 46.1 us
  Pallas kernels  42.6 us (92%)
  local copies, waits for them, and re-layouts  2.22 us (5%)
  between operations  1.29 us (3%)
    pallas_call x1, Pallas kernels, local(): pl.pallas_call(kernel, out_shape=(out, out), in_specs=[anywhere, anywhere...  42.6 us
    unnamed x4, local copies, waits for them, and re-layouts  2.22 us

profile of v1, /device:TPU:1, one launch (start us, length us, event | category | flops | bytes accessed | tf_op | source)
XLA Modules:
  0.0 46.1 jit_solution(16952946185815995021)
XLA Ops:
  1.3 42.6 %shard_map.68 = (f32[32,768]{1,0:T(8,128)}, f32[32,768]{1,0:T(8,128)}) custom-call(bf16[32,768]{1,0:T(8,128)(2,1)} %refs_0_.1, bf16[32,768]{1,0:T(8,128)(2,1)} %refs_1_.1, f32[32]{0:T(128)} %refs_2_.1, f32[512]{0:T(512)} %refs_3_.1, f32[1]{0:T(128)} %bitcast.1.refs_4_), custom_call_target="tpu_custom_call" | custom-call | tf_op jit(solution)/shard_map/pallas_call | solution.py:468
  43.9 0.0 copy-start
  43.9 1.6 %copy.10 = f32[32,768]{1,0:T(8,128)} copy(f32[32,768]{1,0:T(8,128)} %get-tuple-element.4) | data formatting | bytes 196608
  45.5 0.0 copy-done
  45.5 0.6 %copy.11 = f32[32,768]{1,0:T(8,128)} copy(f32[32,768]{1,0:T(8,128)S(1)} %copy-done) | data formatting | bytes 196608
Async XLA Ops:
  43.9 1.6 %copy-start = (f32[32,768]{1,0:T(8,128)S(1)}, f32[32,768]{1,0:T(8,128)}, u32[]{:S(2)}) copy-start(f32[32,768]{1,0:T(8,128)} %get-tuple-element.5) | copy-start | bytes 294916

commit v2 on v1

v2 whole, which is shorter than its diff:
```python
import math

import jax
import jax.numpy as jnp
from jax import lax
from jax.experimental import pallas as pl
from jax.experimental.pallas import tpu as pltpu
from jax.sharding import PartitionSpec as P

MESH = pl.DeviceIdType.MESH
F32, BF16 = jnp.float32, jnp.bfloat16
ROWS = 32
HALF = 16
BATCH = 8192
LOG2E = math.log2(math.e)
TOP = math.log(BATCH) + 3.5
BOUND = 512 * 6.0 * 2.0**-30
TINY = 1e-37


def encode(value, inverse):
    t = value * inverse
    u = t * jnp.abs(t)
    return (u * jnp.abs(u)).astype(BF16)


def decode(coded, scale):
    wide = coded.astype(F32)
    r = lax.rsqrt(jnp.maximum(jnp.abs(wide), TINY))
    return (wide * r) * (r * lax.rsqrt(r)) * scale


def body(
    width,
    q_in, p_in, qn_in, pn_in,
    oq_ref, op_ref,
    q_all, p_all, qn_all, pn_all,
    w_hi, w_lo, g_q, g_p, xq_out, xq_in,
    zs1, zs2, zd_in, zf_in, zh_in, z2_in,
    pa_out, pa_in, pb_out, pb_in,
    fa_out, fa_in, fb_out, fb_in,
    sc_me, sc_q, sc_qr, sc_pa, sc_pb, sx_in, sz_in, sz2_in, sy1_in, sx1_in, sfa_in, sfb_in,
    qn_smem, ssem, lsem, q_sem, qh_sem, qn_sem, pa_sem, pb_sem, pn_sem,
    xq_sem, xs_sem, zd_sem, zf_sem, zh_sem, z2_sem, zsc_sem, zsc2_sem,
    ra_sem, rb_sem, ras_sem, rbs_sem, fa_sem, fb_sem, fas_sem, fbs_sem,
):
    slab, blk = lax.axis_index("slab"), lax.axis_index("blk")

    def ring(value, size):
        return [value] + [lax.rem(value + d, size) for d in range(1, size)]

    x, c = lax.div(slab, 4), lax.rem(slab, 2)
    yl = lax.rem(lax.div(slab, 2), 2)
    z, yh = lax.div(blk, 2), lax.rem(blk, 2)
    y = yh * 2 + yl
    xs, ys, zs = ring(x, 4), ring(y, 4), ring(z, 8)
    in_row, in_block = yl * 2, z * 2 + yh
    y_row = [(lax.rem(yy, 2) * 2, z * 2 + lax.div(yy, 2)) for yy in ys]
    other = 1 - c
    same = c == yh
    partner = (slab + 1 - 2 * c, blk)

    def at_x(d, cc):
        return (xs[d] * 4 + in_row + cc, in_block)

    def at_y(d, cc):
        return (x * 4 + y_row[d][0] + cc, y_row[d][1])

    def at_z(d):
        return (slab, zs[d] * 2 + yh)

    def at_owner(yy, cc):
        return (x * 4 + yy * 2 + cc, z * 2 + c)

    pending = []
    count = [0]

    def send(build, when=None):
        index = count[0]
        count[0] += 1

        def make():
            src, dst, rsem, to = build()
            return pltpu.make_async_remote_copy(
                src_ref=src, dst_ref=dst, send_sem=ssem.at[index], recv_sem=rsem, device_id=to, device_id_type=MESH
            )

        if when is None:
            make().start()
        else:
            pl.when(when)(lambda: make().start())
        pending.append((make, when))

    def wait(dst, rsem):
        pltpu.make_async_remote_copy(
            src_ref=dst, dst_ref=dst, send_sem=lsem.at[0], recv_sem=rsem, device_id=partner, device_id_type=MESH
        ).wait_recv()

    def settle():
        for make, when in pending:
            if when is None:
                make().wait_send()
            else:
                pl.when(when)(lambda make=make: make().wait_send())
        pending.clear()

    barrier = pltpu.get_barrier_semaphore()
    peers = [at_z(d) for d in (2, 6)]
    peers += [at_x(d, cc) for d in (2, 1, 3) for cc in (0, 1)]
    peers += [at_y(d, cc) for d in (2, 1, 3) for cc in (0, 1)]
    peers += [at_z(d) for d in (1, 7)]
    peers += [partner]
    for peer in peers:
        pl.semaphore_signal(barrier, inc=1, device_id=peer, device_id_type=MESH)

    me_q = c * 8 + z
    low, high = pl.ds(0, HALF), pl.ds(HALF, HALF)
    norms = pltpu.make_async_copy(qn_in, qn_smem, lsem.at[2])
    norms.start()
    local_q = pltpu.make_async_copy(q_in, q_all.at[me_q], lsem.at[1])
    local_q.start()

    @pl.when(same)
    def _():
        pltpu.make_async_copy(p_in.at[low], p_all.at[slab, low], pa_sem.at[slab]).start()
        pltpu.make_async_copy(p_in.at[high], p_all.at[slab, high], pb_sem.at[slab]).start()
        pltpu.make_async_copy(pn_in, pn_all.at[0], pn_sem.at[0]).start()

    norms.wait()
    lanes = lax.broadcasted_iota(jnp.int32, (1, 128), 1)
    row = jnp.zeros((1, 128), F32)
    for i in range(ROWS):
        row = jnp.where(lanes == i, qn_smem[i], row)
    qn_all[me_q] = row
    pl.semaphore_wait(barrier, len(peers))

    def own(half, sem, to, when=None):
        send(lambda: (p_in.at[half], p_all.at[slab, half], sem.at[slab], to), when)

    def own_q(to):
        send(lambda: (q_in, q_all.at[me_q], q_sem.at[me_q], to))
        send(lambda: (qn_all.at[me_q], qn_all.at[me_q], qn_sem.at[me_q], to))

    apart = jnp.logical_not(same)
    own(low, pa_sem, partner, apart)
    own(high, pb_sem, partner, apart)
    for d in (2, 6):
        own_q(at_z(d))
    for d in (2, 1, 3):
        own(low, pa_sem, at_x(d, yh))
        own(high, pb_sem, at_y(d, yh))
    own_q(partner)
    for d in (1, 7):
        own_q(at_z(d))
    send(lambda: (pn_in, pn_all.at[0], pn_sem.at[0], at_y(2, c)), same)
    for d in (2, 1, 3):
        own(low, pa_sem, at_y(d, c), same)
        own(high, pb_sem, at_x(d, c), same)

    def relay_a(e, cc, mine=False):
        slot = xs[e] * 4 + in_row + cc

        @pl.when(same)
        def _():
            wait(p_all.at[slot, low], pa_sem.at[slot])

        for d in (2, 1, 3):
            send(lambda d=d: (p_all.at[slot, low], p_all.at[slot, low], pa_sem.at[slot], at_y(d, c)), same)

    def relay_b(yy, cc, when=None):
        slot = x * 4 + yy * 2 + cc
        if when is None:
            wait(p_all.at[slot, high], pb_sem.at[slot])
        else:
            pl.when(when)(lambda: wait(p_all.at[slot, high], pb_sem.at[slot]))
        for d in (2, 1, 3):
            send(lambda d=d: (p_all.at[slot, high], p_all.at[slot, high], pb_sem.at[slot], at_x(d, c)), when)

    relay_a(0, other)
    relay_b(yl, other, same)
    for e in (1, 3):
        for cc in (0, 1):
            relay_a(e, cc)
    for yy in (yl, 1 - yl):
        for cc in (0, 1):
            relay_b(yy, cc, apart if yy is yl else None)
    for cc in (0, 1):
        relay_a(2, cc)

    def q_wait(slot):
        wait(q_all.at[slot], q_sem.at[slot])
        wait(qn_all.at[slot], qn_sem.at[slot])

    def q_send(slot, to):
        send(lambda: (q_all.at[slot], q_all.at[slot], q_sem.at[slot], to))
        send(lambda: (qn_all.at[slot], qn_all.at[slot], qn_sem.at[slot], to))

    for d, near, far, half, hsem in ((6, 1, 2, low, 0), (2, 7, 6, high, 1)):
        slot = c * 8 + zs[d]
        q_wait(slot)
        send(
            lambda slot=slot, half=half, hsem=hsem, far=far: (
                q_all.at[slot, half], q_all.at[slot, half], qh_sem.at[hsem], at_z(far)
            )
        )
        if hsem == 0:
            send(lambda slot=slot, far=far: (qn_all.at[slot], qn_all.at[slot], qn_sem.at[slot], at_z(far)))
        q_send(slot, at_z(near))
        q_send(slot, partner)
    for d in (1, 7, 3, 5):
        slot = c * 8 + zs[d]
        q_wait(slot)
        q_send(slot, partner)
    slot = c * 8 + zs[4]
    wait(q_all.at[slot, low], qh_sem.at[0])
    wait(q_all.at[slot, high], qh_sem.at[1])
    wait(qn_all.at[slot], qn_sem.at[slot])
    q_send(slot, partner)

    for e in range(4):
        for yy in (yl, 1 - yl):
            for cc in (0, 1):
                slot = xs[e] * 4 + yy * 2 + cc

                def lower(slot=slot):
                    wait(p_all.at[slot, low], pa_sem.at[slot])

                if yy is not yl:
                    lower()
                else:
                    pl.when(apart)(lower)
                if e:
                    wait(p_all.at[slot, high], pb_sem.at[slot])

    @pl.when(same)
    def _():
        wait(p_all.at[slab, low], pa_sem.at[slab])
        wait(p_all.at[slab, high], pb_sem.at[slab])

    for d in range(8):
        q_wait(other * 8 + zs[d])
    local_q.wait()
    wait(pn_all.at[0], pn_sem.at[0])

    scale = 2.0 / math.sqrt(width)
    columns = pn_all.shape[1]
    b = jnp.exp(TOP - pn_all[...])
    a_t = jnp.exp(TOP - qn_all[...].reshape(16, 128)).T
    passages = p_all[...].reshape(columns, width)
    largest = jnp.zeros((8, 128), F32)
    column = lax.broadcasted_iota(jnp.int32, (ROWS, columns), 1) - lax.broadcasted_iota(jnp.int32, (ROWS, columns), 0)
    for chunk in range(4):
        rows = q_all[pl.ds(chunk * 4, 4)].reshape(4 * ROWS, width)
        scores = lax.dot_general(rows, passages, (((1,), (1,)), ((), ())), preferred_element_type=F32)
        terms = jnp.exp2(scores * (scale * LOG2E) - TOP * LOG2E)
        for k in range(4):
            slot = chunk * 4 + k
            first = ((x * 4 + yl * 2 + slot // 8) * 16 + (slot % 8) * 2 + yh) * ROWS - (z * 2 + c) * columns
            here = slice(k * ROWS, (k + 1) * ROWS)
            weights = terms[here] * (a_t[:ROWS, slot : slot + 1] + b) - jnp.where(column == first, 2.0, 0.0)
            top = weights.astype(BF16)
            at = pl.ds(slot * ROWS, ROWS)
            w_hi[at, :] = top
            w_lo[at, :] = (weights - top.astype(F32)).astype(BF16)
            size = jnp.abs(weights)
            size = jnp.maximum(size[:HALF], size[HALF:])
            size = jnp.maximum(size[:8], size[8:])
            for j in range(columns // 128):
                largest = jnp.maximum(largest, size[:, j * 128 : (j + 1) * 128])
    mine = jnp.maximum(jnp.max(largest, axis=(0, 1), keepdims=True), 1e-30) * BOUND
    mine = jnp.broadcast_to(mine, (1, 128))
    sc_me[0] = mine
    row_of = [2 * c + yy for yy in (0, 1)]
    far_row = [row != y for row in row_of]
    back_a = [lax.rem(y - row + 3 + 4, 4) for row in row_of]
    back_b = [lax.rem(y - row + 4, 4) for row in row_of]
    send(lambda: (sc_me.at[0], sx_in.at[0], xs_sem.at[0], partner))
    for d in (2, 1, 3):
        send(lambda d=d: (sc_me.at[0], sx1_in.at[3 - d], rbs_sem.at[3 - d], at_x(d, c)))
    for yy in (0, 1):
        send(
            lambda yy=yy: (sc_me.at[0], sy1_in.at[back_a[yy]], ras_sem.at[back_a[yy]], at_owner(yy, c)),
            far_row[yy],
        )

    def lane(row):
        return row[:, :1]

    inverse = lane(1.0 / mine)

    for chunk in range(2):
        at = pl.ds(pl.multiple_of(other * 8 * ROWS + chunk * 4 * ROWS, 4 * ROWS), 4 * ROWS)
        part = jnp.dot(w_hi[at, :], passages, preferred_element_type=F32)
        part += jnp.dot(w_lo[at, :], passages, preferred_element_type=F32)
        to = pl.ds(chunk * 4, 4)
        xq_out[to] = part.reshape(4, ROWS, width)
        send(lambda to=to, chunk=chunk: (xq_out.at[to], xq_in.at[to], xq_sem.at[chunk], partner))
    for chunk in range(2):
        at = pl.ds(pl.multiple_of(c * 8 * ROWS + chunk * 4 * ROWS, 4 * ROWS), 4 * ROWS)
        part = jnp.dot(w_hi[at, :], passages, preferred_element_type=F32)
        part += jnp.dot(w_lo[at, :], passages, preferred_element_type=F32)
        g_q[pl.ds(chunk * 4, 4)] = part.reshape(4, ROWS, width)

    queries = q_all[...].reshape(16 * ROWS, width)
    across = (((0,), (0,)), ((), ()))

    def passage_chunk(d):
        xm = xs[d]
        at = pl.ds(pl.multiple_of(xm * 4 * ROWS, 4 * ROWS), 4 * ROWS)
        part = lax.dot_general(w_hi[:, at], queries, across, preferred_element_type=F32)
        part += lax.dot_general(w_lo[:, at], queries, across, preferred_element_type=F32)
        part = part.reshape(2, 2, ROWS, width)
        g_p[xm] = part
        for yy in (0, 1):
            coded = encode(part[yy], inverse)
            pa_out[yy, xm] = coded[:, :HALF]
            if d:
                pb_out[3 - d, yy] = coded[:, HALF:]
                send(lambda yy=yy: (pb_out.at[3 - d, yy], pb_in.at[3 - d, yy], rb_sem.at[3 - d, yy], at_x(d, c)))
            send(
                lambda yy=yy: (pa_out.at[yy, xm], pa_in.at[back_a[yy], xm], ra_sem.at[back_a[yy], xm], at_owner(yy, c)),
                far_row[yy],
            )

    passage_chunk(2)

    wait(sx_in.at[0], xs_sem.at[0])
    both = mine + sx_in[0]
    sc_q[0] = both
    for chunk in range(2):
        wait(xq_in.at[pl.ds(chunk * 4, 4)], xq_sem.at[chunk])
    for d in (1, 2, 6, 7):
        send(lambda d=d: (sc_q.at[0], sz_in.at[8 - d], zsc_sem.at[8 - d], at_z(d)))
    inverse_q = lane(1.0 / both)

    def column_sum(zz):
        return g_q[zz] + xq_in[zz]

    far = encode(column_sum(zs[4]), inverse_q)
    zs1[4, low] = far[:HALF]
    zs1[4, high] = far[HALF:]
    for i, d in enumerate((5, 3)):
        zs1[i] = encode(column_sum(zs[d]), inverse_q)
    for i, d in enumerate((1, 7)):
        zs1[2 + i] = encode(column_sum(zs[d]), inverse_q)
    send(lambda: (zs1.at[4, low], zh_in.at[0], zh_sem.at[0], at_z(6)))
    send(lambda: (zs1.at[4, high], zh_in.at[1], zh_sem.at[1], at_z(2)))
    send(lambda: (zs1.at[0], zf_in.at[0], zf_sem.at[0], at_z(7)))
    send(lambda: (zs1.at[1], zf_in.at[1], zf_sem.at[1], at_z(1)))
    send(lambda: (zs1.at[2], zd_in.at[0], zd_sem.at[0], at_z(1)))
    send(lambda: (zs1.at[3], zd_in.at[1], zd_sem.at[1], at_z(7)))

    for d in (1, 3, 0):
        passage_chunk(d)

    settle()

    def relay_rows():
        for d in (1, 2, 6, 7):
            wait(sz_in.at[d], zsc_sem.at[d])
        for i in (0, 1):
            near, far_ = (1, 2) if i == 0 else (7, 6)
            to = at_z(6 if i == 0 else 2)
            wait(zh_in.at[i], zh_sem.at[i])
            wait(zf_in.at[i], zf_sem.at[i])
            total = both + sz_in[near] + sz_in[far_]
            sc_qr[i] = total
            value = column_sum(zs[6 if i == 0 else 2]) + decode(zf_in[i], lane(sz_in[near]))
            extra = decode(zh_in[i], lane(sz_in[far_]))
            inv = lane(1.0 / total)
            first_half, second_half = value[:HALF], value[HALF:]
            if i == 0:
                first_half = first_half + extra
            else:
                second_half = second_half + extra
            zs2[i, low] = encode(first_half, inv)
            zs2[i, high] = encode(second_half, inv)
            send(lambda i=i, to=to: (sc_qr.at[i], sz2_in.at[i], zsc2_sem.at[i], to))
            send(lambda i=i, to=to: (zs2.at[i], z2_in.at[i], z2_sem.at[i], to))

    total_b = []

    def relay_upper(yy):
        if not total_b:
            for d in (1, 2, 3):
                wait(sx1_in.at[d - 1], rbs_sem.at[d - 1])
            total_b.append(mine + sx1_in[0] + sx1_in[1] + sx1_in[2])
            sc_pb[0] = total_b[0]
        inv_b = lane(1.0 / total_b[0])
        for d in (2, 1, 3):
            wait(pb_in.at[d - 1, yy], rb_sem.at[d - 1, yy])
        for cc in (0, 1):
            value = g_p[x, yy, cc, HALF:]
            for d in (2, 1, 3):
                value = value + decode(pb_in[d - 1, yy, cc], lane(sx1_in[d - 1]))
            fb_out[yy, cc] = encode(value, inv_b)
        for cc in (0, 1):
            mine_too = jnp.logical_and(jnp.logical_not(far_row[yy]), c == cc)

            @pl.when(mine_too)
            def _(cc=cc):
                fb_in[0] = fb_out[yy, cc]
                sfb_in[0] = total_b[0]

            away = jnp.logical_not(mine_too)
            back, to = back_b[yy], at_owner(yy, cc)
            send(lambda: (sc_pb.at[0], sfb_in.at[back], fbs_sem.at[back], to), away)
            send(lambda cc=cc, back=back, to=to: (fb_out.at[yy, cc], fb_in.at[back], fb_sem.at[back], to), away)

    def relay_lower(e):
        xm = xs[e]

        @pl.when(same)
        def _():
            if e == 2:
                for d in (1, 2, 3):
                    wait(sy1_in.at[d - 1], ras_sem.at[d - 1])
                sc_pa[0] = mine + sy1_in[0] + sy1_in[1] + sy1_in[2]
            inv_a = lane(1.0 / sc_pa[0])
            for d in (1, 2, 3):
                wait(pa_in.at[d - 1, xm], ra_sem.at[d - 1, xm])
            for cc in (0, 1):
                value = g_p[xm, yl, cc, :HALF]
                for d in (1, 2, 3):
                    value = value + decode(pa_in[d - 1, xm, cc], lane(sy1_in[d - 1]))
                fa_out[e, cc] = encode(value, inv_a)
            if e == 0:
                fa_in[0] = fa_out[0, c]
                sfa_in[0] = sc_pa[0]

        if e:
            back = 4 - e
            for cc in (0, 1):
                send(lambda cc=cc: (sc_pa.at[0], sfa_in.at[back], fas_sem.at[back], at_x(e, cc)), same)
                send(lambda cc=cc: (fa_out.at[e, cc], fa_in.at[back], fa_sem.at[back], at_x(e, cc)), same)
        else:
            send(lambda: (sc_pa.at[0], sfa_in.at[0], fas_sem.at[0], partner), same)
            send(lambda: (fa_out.at[0, other], fa_in.at[0], fa_sem.at[0], partner), same)

    relay_lower(2)
    relay_lower(1)
    relay_rows()
    relay_upper(0)
    relay_lower(3)
    relay_upper(1)
    relay_lower(0)

    value = column_sum(z)
    for i, d in ((0, 7), (1, 1)):
        wait(zd_in.at[i], zd_sem.at[i])
        value = value + decode(zd_in[i], lane(sz_in[d]))
    for i in (0, 1):
        wait(sz2_in.at[i], zsc2_sem.at[i])
        wait(z2_in.at[i], z2_sem.at[i])
        value = value + decode(z2_in[i], lane(sz2_in[i]))
    oq_ref[...] = value

    for parts, scales, psem, sem, half in ((fb_in, sfb_in, fb_sem, fbs_sem, high), (fa_in, sfa_in, fa_sem, fas_sem, low)):
        for e in range(4):

            def arrived(e=e, parts=parts, scales=scales, psem=psem, sem=sem):
                wait(scales.at[e], sem.at[e])
                wait(parts.at[e], psem.at[e])

            if e:
                arrived()
            else:
                pl.when(jnp.logical_not(same))(arrived)
        value = decode(parts[0], lane(scales[0]))
        for e in (1, 2, 3):
            value = value + decode(parts[e], lane(scales[e]))
        op_ref[half, :] = value

    settle()


N_SENDS = 220
VMEM_LIMIT = 20 * 2**20


def local(queries, passages, query_lognorm, passage_lognorm, loss_cotangent):
    width = queries.shape[1]
    columns = passage_lognorm.shape[0]
    dma = pltpu.SemaphoreType.DMA
    vm = pltpu.VMEM
    scratch = [
        vm((16, ROWS, width), BF16), vm((16, ROWS, width), BF16), vm((16, 1, 128), F32), vm((1, columns), F32),
        vm((16 * ROWS, columns), BF16), vm((16 * ROWS, columns), BF16),
        vm((8, ROWS, width), F32), vm((4, 2, 2, ROWS, width), F32),
        vm((8, ROWS, width), F32), vm((8, ROWS, width), F32),
        vm((5, ROWS, width), BF16), vm((2, ROWS, width), BF16), vm((2, ROWS, width), BF16),
        vm((2, ROWS, width), BF16), vm((2, HALF, width), BF16), vm((2, ROWS, width), BF16),
        vm((2, 4, 2, HALF, width), BF16), vm((3, 4, 2, HALF, width), BF16),
        vm((3, 2, 2, HALF, width), BF16), vm((3, 2, 2, HALF, width), BF16),
        vm((4, 2, HALF, width), BF16), vm((4, HALF, width), BF16),
        vm((2, 2, HALF, width), BF16), vm((4, HALF, width), BF16),
        *[vm((n, 1, 128), F32) for n in (1, 1, 2, 1, 1, 1, 8, 2, 3, 3, 4, 4)],
        pltpu.SMEM((ROWS,), F32), dma((N_SENDS,)), dma((3,)), dma((16,)), dma((2,)), dma((16,)), dma((16,)), dma((16,)), dma((1,)),
        dma((2,)), dma((1,)), dma((2,)), dma((2,)), dma((2,)), dma((2,)), dma((8,)), dma((2,)),
        dma((3, 4)), dma((3, 2)), dma((3,)), dma((3,)), dma((4,)), dma((4,)), dma((4,)), dma((4,)),
    ]
    out = jax.ShapeDtypeStruct(queries.shape, F32)
    vmem = pl.BlockSpec(memory_space=pltpu.VMEM)

    def kernel(*refs):
        body(width, *refs)

    sums = pl.pallas_call(
        kernel,
        out_shape=(out, out),
        in_specs=[pl.BlockSpec(memory_space=pltpu.HBM)] * 4,
        out_specs=[vmem] * 2,
        scratch_shapes=scratch,
        compiler_params=pltpu.CompilerParams(collective_id=0, has_side_effects=True, vmem_limit_bytes=VMEM_LIMIT),
    )(*[pltpu.with_memory_space_constraint(v, pltpu.HBM) for v in (queries, passages, query_lognorm, passage_lognorm)])

    factor = loss_cotangent * (1.0 / math.sqrt(width))
    return sums[0] * factor, sums[1] * factor


def solution(mesh):
    return jax.shard_map(
        local,
        mesh=mesh,
        in_specs=(
            P(("slab", "blk"), None),
            P(("blk", "slab"), None),
            P(("slab", "blk")),
            P("blk"),
            P(),
        ),
        out_specs=(P(("slab", "blk"), None), P(("blk", "slab"), None)),
        check_vma=False,
    )
```

time: 46.3 us -> 39.5 us (0.85)
  Pallas kernels: 42.6 us -> 37.4 us
  local copies, waits for them, and re-layouts: 2.22 us -> 0 us
  other arithmetic: 0 us -> 0.69 us
    pallas_call x1, Pallas kernels: 42.6 us -> 37.4 us  [local(): pl.pallas_call(kernel, out_shape=(out, out), in_specs=[pl.BlockSpec(memor...]
    unnamed x4 -> x0, local copies, waits for them, and re-layouts: 2.22 us -> none
    mul x0 -> x1, other arithmetic: none -> 0.69 us  [local(): return (sums[0] * factor, sums[1] * factor)]
where the time goes in v2:
time: 39.5 us; the launch traced here: 39.4 us
  Pallas kernels  37.4 us (95%)
  between operations  1.29 us (3%)
  other arithmetic  0.69 us (2%)
    pallas_call x1, Pallas kernels, local(): pl.pallas_call(kernel, out_shape=(out, out), in_specs=[pl.BlockSpec(memor...  37.4 us

profile of v2, /device:TPU:1, one launch (start us, length us, event | category | flops | bytes accessed | tf_op | source)
XLA Modules:
  0.0 39.4 jit_solution(7400697779466684079)
XLA Ops:
  1.3 37.4 %shard_map.68 = (f32[32,768]{1,0:T(8,128)S(1)}, f32[32,768]{1,0:T(8,128)S(1)}) custom-call(bf16[32,768]{1,0:T(8,128)(2,1)} %refs_0_.1, bf16[32,768]{1,0:T(8,128)(2,1)} %refs_1_.1, f32[32]{0:T(128)} %refs_2_.1, f32[512]{0:T(512)} %refs_3_.1), custom_call_target="tpu_custom_call" | custom-call | tf_op jit(solution)/shard_map/pallas_call | solution.py:508
  38.7 0.7 %broadcast_multiply_fusion = (f32[32,768]{1,0:T(8,128)}, f32[32,768]{1,0:T(8,128)}) fusion(f32[32,768]{1,0:T(8,128)S(1)} %get-tuple-element.5, f32[]{:T(128)S(6)} %mul.13, f32[32,768]{1,0:T(8,128)S(1)} %get-tuple-element.4), kind=kLoop, calls=%fused_computation | loop fusion | flops 49152 | bytes 393220 | tf_op jit(solution)/shard_map/mul | solution.py:518

commit v3 on v2

--- a/solution.py
+++ b/solution.py
@@ -34,13 +34,13 @@
     width,
     q_in, p_in, qn_in, pn_in,
     oq_ref, op_ref,
-    q_all, p_all, qn_all, pn_all,
+    q_all, p_all, p_own, qn_all, pn_all,
     w_hi, w_lo, g_q, g_p, xq_out, xq_in,
     zs1, zs2, zd_in, zf_in, zh_in, z2_in,
     pa_out, pa_in, pb_out, pb_in,
     fa_out, fa_in, fb_out, fb_in,
     sc_me, sc_q, sc_qr, sc_pa, sc_pb, sx_in, sz_in, sz2_in, sy1_in, sx1_in, sfa_in, sfb_in,
-    qn_smem, ssem, lsem, q_sem, qh_sem, qn_sem, pa_sem, pb_sem, pn_sem,
+    qn_smem, ssem, lsem, q_sem, qn_sem, pa_sem, pb_sem, pn_sem,
     xq_sem, xs_sem, zd_sem, zf_sem, zh_sem, z2_sem, zsc_sem, zsc2_sem,
     ra_sem, rb_sem, ras_sem, rbs_sem, fa_sem, fb_sem, fas_sem, fbs_sem,
 ):
@@ -74,10 +74,15 @@
 
     pending = []
     count = [0]
+    free = []
 
     def send(build, when=None):
-        index = count[0]
-        count[0] += 1
+        if free:
+            index = free.pop(0)
+        else:
+            index = count[0]
+            count[0] += 1
+            assert index < N_SENDS
 
         def make():
             src, dst, rsem, to = build()
@@ -89,36 +94,40 @@
             make().start()
         else:
             pl.when(when)(lambda: make().start())
-        pending.append((make, when))
+        pending.append((make, when, index))
 
     def wait(dst, rsem):
         pltpu.make_async_remote_copy(
             src_ref=dst, dst_ref=dst, send_sem=lsem.at[0], recv_sem=rsem, device_id=partner, device_id_type=MESH
         ).wait_recv()
 
-    def settle():
-        for make, when in pending:
+    def settle(first=None):
+        first = len(pending) if first is None else first
+        for make, when, index in pending[:first]:
             if when is None:
                 make().wait_send()
             else:
                 pl.when(when)(lambda make=make: make().wait_send())
-        pending.clear()
-
+            free.append(index)
+        del pending[:first]
+
+    me_q = c * 8 + z
+    low, high = pl.ds(0, HALF), pl.ds(HALF, HALF)
+    halves = (low, high)
+    norms = pltpu.make_async_copy(qn_in, qn_smem, lsem.at[2])
+    local_q = pltpu.make_async_copy(q_in, q_all.at[me_q], lsem.at[1])
+    local_p = pltpu.make_async_copy(p_in, p_own, lsem.at[3])
+    local_p.start()
+    local_q.start()
+    norms.start()
     barrier = pltpu.get_barrier_semaphore()
-    peers = [at_z(d) for d in (2, 6)]
-    peers += [at_x(d, cc) for d in (2, 1, 3) for cc in (0, 1)]
-    peers += [at_y(d, cc) for d in (2, 1, 3) for cc in (0, 1)]
-    peers += [at_z(d) for d in (1, 7)]
+    peers = [at_x(2, cc) for cc in (0, 1)] + [at_y(2, cc) for cc in (0, 1)]
+    peers += [at_x(d, cc) for d in (1, 3) for cc in (0, 1)]
+    peers += [at_y(d, cc) for d in (1, 3) for cc in (0, 1)]
+    peers += [at_z(d) for d in Z_PEERS]
     peers += [partner]
     for peer in peers:
         pl.semaphore_signal(barrier, inc=1, device_id=peer, device_id_type=MESH)
-
-    me_q = c * 8 + z
-    low, high = pl.ds(0, HALF), pl.ds(HALF, HALF)
-    norms = pltpu.make_async_copy(qn_in, qn_smem, lsem.at[2])
-    norms.start()
-    local_q = pltpu.make_async_copy(q_in, q_all.at[me_q], lsem.at[1])
-    local_q.start()
 
     @pl.when(same)
     def _():
@@ -126,45 +135,55 @@
         pltpu.make_async_copy(p_in.at[high], p_all.at[slab, high], pb_sem.at[slab]).start()
         pltpu.make_async_copy(pn_in, pn_all.at[0], pn_sem.at[0]).start()
 
+    local_p.wait()
+    local_q.wait()
+    pl.semaphore_wait(barrier, len(peers))
+
+    def own(half, sem, to, when=None):
+        send(lambda: (p_own.at[half], p_all.at[slab, half], sem.at[slab], to), when)
+
+    def q_send(slot, h, to):
+        send(lambda: (q_all.at[slot, halves[h]], q_all.at[slot, halves[h]], q_sem.at[slot, h], to))
+
+    def n_send(slot, to):
+        send(lambda: (qn_all.at[slot], qn_all.at[slot], qn_sem.at[slot], to))
+
+    apart = jnp.logical_not(same)
+    own(low, pa_sem, partner, apart)
+    own(high, pb_sem, partner, apart)
+    q_send(me_q, 0, at_z(2))
+    q_send(me_q, 1, at_z(6))
+    for d in (1, 3):
+        own(low, pa_sem, at_x(d, yh))
+        own(high, pb_sem, at_y(d, yh))
+    q_send(me_q, 1, at_z(2))
+    q_send(me_q, 0, at_z(6))
+    for d in (1, 7):
+        q_send(me_q, 0, at_z(d))
+        q_send(me_q, 1, at_z(d))
+    own(low, pa_sem, at_x(2, yh))
+    own(high, pb_sem, at_y(2, yh))
+    for d in (1, 3, 2):
+        own(low, pa_sem, at_y(d, c), same)
+        own(high, pb_sem, at_x(d, c), same)
+    q_send(me_q, 0, partner)
+    q_send(me_q, 1, partner)
+    send(lambda: (pn_in, pn_all.at[0], pn_sem.at[0], at_y(2, c)), same)
     norms.wait()
     lanes = lax.broadcasted_iota(jnp.int32, (1, 128), 1)
     row = jnp.zeros((1, 128), F32)
     for i in range(ROWS):
         row = jnp.where(lanes == i, qn_smem[i], row)
     qn_all[me_q] = row
-    pl.semaphore_wait(barrier, len(peers))
-
-    def own(half, sem, to, when=None):
-        send(lambda: (p_in.at[half], p_all.at[slab, half], sem.at[slab], to), when)
-
-    def own_q(to):
-        send(lambda: (q_in, q_all.at[me_q], q_sem.at[me_q], to))
-        send(lambda: (qn_all.at[me_q], qn_all.at[me_q], qn_sem.at[me_q], to))
-
-    apart = jnp.logical_not(same)
-    own(low, pa_sem, partner, apart)
-    own(high, pb_sem, partner, apart)
-    for d in (2, 6):
-        own_q(at_z(d))
-    for d in (2, 1, 3):
-        own(low, pa_sem, at_x(d, yh))
-        own(high, pb_sem, at_y(d, yh))
-    own_q(partner)
-    for d in (1, 7):
-        own_q(at_z(d))
-    send(lambda: (pn_in, pn_all.at[0], pn_sem.at[0], at_y(2, c)), same)
-    for d in (2, 1, 3):
-        own(low, pa_sem, at_y(d, c), same)
-        own(high, pb_sem, at_x(d, c), same)
-
-    def relay_a(e, cc, mine=False):
+
+    def relay_a(e, cc):
         slot = xs[e] * 4 + in_row + cc
 
         @pl.when(same)
         def _():
             wait(p_all.at[slot, low], pa_sem.at[slot])
 
-        for d in (2, 1, 3):
+        for d in (1, 3, 2):
             send(lambda d=d: (p_all.at[slot, low], p_all.at[slot, low], pa_sem.at[slot], at_y(d, c)), same)
 
     def relay_b(yy, cc, when=None):
@@ -173,9 +192,36 @@
             wait(p_all.at[slot, high], pb_sem.at[slot])
         else:
             pl.when(when)(lambda: wait(p_all.at[slot, high], pb_sem.at[slot]))
-        for d in (2, 1, 3):
+        for d in (1, 3, 2):
             send(lambda d=d: (p_all.at[slot, high], p_all.at[slot, high], pb_sem.at[slot], at_x(d, c)), when)
 
+    def q_wait(slot, h):
+        wait(q_all.at[slot, halves[h]], q_sem.at[slot, h])
+
+    def n_wait(slot):
+        wait(qn_all.at[slot], qn_sem.at[slot])
+
+    def hop(k, h, to_right):
+        slot = c * 8 + zs[8 - k if to_right else k]
+        q_wait(slot, h)
+        if k == 2:
+            if h == (0 if to_right else 1):
+                q_send(slot, h, at_z(2 if to_right else 6))
+            q_send(slot, h, at_z(1 if to_right else 7))
+        q_send(slot, h, partner)
+
+    def norm_hop(k, to_right):
+        slot = c * 8 + zs[8 - k if to_right else k]
+        n_wait(slot)
+        if k == 2:
+            if to_right:
+                n_send(slot, at_z(2))
+            n_send(slot, at_z(1 if to_right else 7))
+        n_send(slot, partner)
+
+    for to in (at_z(2), at_z(6), at_z(1), at_z(7), partner):
+        n_send(me_q, to)
+    early = len(pending)
     relay_a(0, other)
     relay_b(yl, other, same)
     for e in (1, 3):
@@ -184,38 +230,23 @@
     for yy in (yl, 1 - yl):
         for cc in (0, 1):
             relay_b(yy, cc, apart if yy is yl else None)
+    hop(2, 0, True)
+    hop(2, 1, False)
     for cc in (0, 1):
         relay_a(2, cc)
-
-    def q_wait(slot):
-        wait(q_all.at[slot], q_sem.at[slot])
-        wait(qn_all.at[slot], qn_sem.at[slot])
-
-    def q_send(slot, to):
-        send(lambda: (q_all.at[slot], q_all.at[slot], q_sem.at[slot], to))
-        send(lambda: (qn_all.at[slot], qn_all.at[slot], qn_sem.at[slot], to))
-
-    for d, near, far, half, hsem in ((6, 1, 2, low, 0), (2, 7, 6, high, 1)):
-        slot = c * 8 + zs[d]
-        q_wait(slot)
-        send(
-            lambda slot=slot, half=half, hsem=hsem, far=far: (
-                q_all.at[slot, half], q_all.at[slot, half], qh_sem.at[hsem], at_z(far)
-            )
-        )
-        if hsem == 0:
-            send(lambda slot=slot, far=far: (qn_all.at[slot], qn_all.at[slot], qn_sem.at[slot], at_z(far)))
-        q_send(slot, at_z(near))
-        q_send(slot, partner)
-    for d in (1, 7, 3, 5):
-        slot = c * 8 + zs[d]
-        q_wait(slot)
-        q_send(slot, partner)
-    slot = c * 8 + zs[4]
-    wait(q_all.at[slot, low], qh_sem.at[0])
-    wait(q_all.at[slot, high], qh_sem.at[1])
-    wait(qn_all.at[slot], qn_sem.at[slot])
-    q_send(slot, partner)
+    hop(2, 1, True)
+    hop(2, 0, False)
+    norm_hop(2, True)
+    norm_hop(2, False)
+    settle(early)
+    for k in (1, 3):
+        for right in (True, False):
+            for h in (0, 1) if right else (1, 0):
+                hop(k, h, right)
+            norm_hop(k, right)
+    hop(4, 0, True)
+    hop(4, 1, False)
+    norm_hop(4, True)
 
     for e in range(4):
         for yy in (yl, 1 - yl):
@@ -237,9 +268,11 @@
         wait(p_all.at[slab, low], pa_sem.at[slab])
         wait(p_all.at[slab, high], pb_sem.at[slab])
 
-    for d in range(8):
-        q_wait(other * 8 + zs[d])
-    local_q.wait()
+    for d in (0, 1, 7, 2, 6, 3, 5, 4):
+        slot = other * 8 + zs[d]
+        q_wait(slot, 0)
+        q_wait(slot, 1)
+        n_wait(slot)
     wait(pn_all.at[0], pn_sem.at[0])
 
     scale = 2.0 / math.sqrt(width)
@@ -269,6 +302,7 @@
                 largest = jnp.maximum(largest, size[:, j * 128 : (j + 1) * 128])
     mine = jnp.maximum(jnp.max(largest, axis=(0, 1), keepdims=True), 1e-30) * BOUND
     mine = jnp.broadcast_to(mine, (1, 128))
+    settle()
     sc_me[0] = mine
     row_of = [2 * c + yy for yy in (0, 1)]
     far_row = [row != y for row in row_of]
@@ -474,7 +508,8 @@
     settle()
 
 
-N_SENDS = 220
+N_SENDS = 81
+Z_PEERS = (2, 6, 1, 7)
 VMEM_LIMIT = 20 * 2**20
 
 
@@ -484,7 +519,7 @@
     dma = pltpu.SemaphoreType.DMA
     vm = pltpu.VMEM
     scratch = [
-        vm((16, ROWS, width), BF16), vm((16, ROWS, width), BF16), vm((16, 1, 128), F32), vm((1, columns), F32),
+        vm((16, ROWS, width), BF16), vm((16, ROWS, width), BF16), vm((ROWS, width), BF16), vm((16, 1, 128), F32), vm((1, columns), F32),
         vm((16 * ROWS, columns), BF16), vm((16 * ROWS, columns), BF16),
         vm((8, ROWS, width), F32), vm((4, 2, 2, ROWS, width), F32),
         vm((8, ROWS, width), F32), vm((8, ROWS, width), F32),
@@ -495,7 +530,7 @@
         vm((4, 2, HALF, width), BF16), vm((4, HALF, width), BF16),
         vm((2, 2, HALF, width), BF16), vm((4, HALF, width), BF16),
         *[vm((n, 1, 128), F32) for n in (1, 1, 2, 1, 1, 1, 8, 2, 3, 3, 4, 4)],
-        pltpu.SMEM((ROWS,), F32), dma((N_SENDS,)), dma((3,)), dma((16,)), dma((2,)), dma((16,)), dma((16,)), dma((16,)), dma((1,)),
+        pltpu.SMEM((ROWS,), F32), dma((N_SENDS,)), dma((4,)), dma((16, 2)), dma((16,)), dma((16,)), dma((16,)), dma((1,)),
         dma((2,)), dma((1,)), dma((2,)), dma((2,)), dma((2,)), dma((2,)), dma((8,)), dma((2,)),
         dma((3, 4)), dma((3, 2)), dma((3,)), dma((3,)), dma((4,)), dma((4,)), dma((4,)), dma((4,)),
     ]
@@ -514,7 +549,8 @@
         compiler_params=pltpu.CompilerParams(collective_id=0, has_side_effects=True, vmem_limit_bytes=VMEM_LIMIT),
     )(*[pltpu.with_memory_space_constraint(v, pltpu.HBM) for v in (queries, passages, query_lognorm, passage_lognorm)])
 
-    factor = loss_cotangent * (1.0 / math.sqrt(width))
+    sums = lax.optimization_barrier((sums[0], sums[1], loss_cotangent))
+    factor = sums[2] * (1.0 / math.sqrt(width))
     return sums[0] * factor, sums[1] * factor
 
 

time: 39.5 us -> 37.7 us (0.954)
  Pallas kernels: 37.4 us -> 35.5 us
    pallas_call x1, Pallas kernels: 37.4 us -> 35.5 us  [local(): pl.pallas_call(kernel, out_shape=(out, out), in_specs=[pl.BlockSpec(memor...]
where the time goes in v3:
time: 37.7 us; the launch traced here: 37.5 us
  Pallas kernels  35.5 us (94%)
  between operations  1.29 us (3%)
  other arithmetic  0.69 us (2%)
    pallas_call x1, Pallas kernels, local(): pl.pallas_call(kernel, out_shape=(out, out), in_specs=[pl.BlockSpec(memor...  35.5 us

profile of v3, /device:TPU:1, one launch (start us, length us, event | category | flops | bytes accessed | tf_op | source)
XLA Modules:
  0.0 37.5 jit_solution(6513254203848901800)
XLA Ops:
  1.3 35.5 %shard_map.68 = (f32[32,768]{1,0:T(8,128)S(1)}, f32[32,768]{1,0:T(8,128)S(1)}) custom-call(bf16[32,768]{1,0:T(8,128)(2,1)} %refs_0_.1, bf16[32,768]{1,0:T(8,128)(2,1)} %refs_1_.1, f32[32]{0:T(128)} %refs_2_.1, f32[512]{0:T(512)} %refs_3_.1), custom_call_target="tpu_custom_call" | custom-call | tf_op jit(solution)/shard_map/pallas_call | solution.py:543
  36.8 0.7 %broadcast_multiply_fusion = (f32[32,768]{1,0:T(8,128)}, f32[32,768]{1,0:T(8,128)}) fusion(f32[32,768]{1,0:T(8,128)S(1)} %get-tuple-element.11, f32[]{:T(128)S(6)} %mul.13, f32[32,768]{1,0:T(8,128)S(1)} %get-tuple-element.9), kind=kLoop, calls=%fused_computation | loop fusion | flops 49152 | bytes 393220 | tf_op jit(solution)/shard_map/mul | solution.py:554

commit v4 on v3

v4 whole, which is shorter than its diff:
```python
import math

import jax
import jax.numpy as jnp
from jax import lax
from jax.experimental import pallas as pl
from jax.experimental.pallas import tpu as pltpu
from jax.sharding import PartitionSpec as P

MESH = pl.DeviceIdType.MESH
F32, BF16 = jnp.float32, jnp.bfloat16
ROWS = 32
HALF = 16
BATCH = 8192
LOG2E = math.log2(math.e)
TOP = math.log(BATCH) + 3.5
BOUND = 512 * 6.0 * 2.0**-30
TINY = 1e-37


def encode(value, inverse):
    t = value * inverse
    u = t * jnp.abs(t)
    return (u * jnp.abs(u)).astype(BF16)


def decode(coded, scale):
    wide = coded.astype(F32)
    r = lax.rsqrt(jnp.maximum(jnp.abs(wide), TINY))
    return (wide * r) * (r * lax.rsqrt(r)) * scale


def body(
    width,
    q_in, p_in, qn_in, pn_in,
    oq_ref, op_ref,
    q_all, p_all, p_own, qn_all, pn_all,
    w_hi, w_lo, g_q, g_p, xq_out, xq_in,
    zs1, zs2, zd_in, zf_in, zh_in, z2_in,
    pa_out, pa_in, pb_out, pb_in,
    fa_out, fa_in, fb_out, fb_in,
    sc_me, sc_q, sc_qr, sc_pa, sc_pb, sx_in, sz_in, sz2_in, sy1_in, sx1_in, sfa_in, sfb_in,
    spare, qn_smem, ssem, lsem, q_sem, qn_sem, pa_sem, pb_sem, pn_sem,
    xq_sem, xs_sem, zd_sem, zr_sem, z2_sem, zsc_sem, zsc2_sem,
    ra_sem, rb_sem, ras_sem, rbs_sem, fa_sem, fb_sem, fas_sem, fbs_sem,
):
    slab, blk = lax.axis_index("slab"), lax.axis_index("blk")

    def ring(value, size):
        return [value] + [lax.rem(value + d, size) for d in range(1, size)]

    x, c = lax.div(slab, 4), lax.rem(slab, 2)
    yl = lax.rem(lax.div(slab, 2), 2)
    z, yh = lax.div(blk, 2), lax.rem(blk, 2)
    y = yh * 2 + yl
    xs, ys, zs = ring(x, 4), ring(y, 4), ring(z, 8)
    in_row, in_block = yl * 2, z * 2 + yh
    y_row = [(lax.rem(yy, 2) * 2, z * 2 + lax.div(yy, 2)) for yy in ys]
    other = 1 - c
    same = c == yh
    partner = (slab + 1 - 2 * c, blk)

    def at_x(d, cc):
        return (xs[d] * 4 + in_row + cc, in_block)

    def at_y(d, cc):
        return (x * 4 + y_row[d][0] + cc, y_row[d][1])

    def at_z(d):
        return (slab, zs[d] * 2 + yh)

    def at_owner(yy, cc):
        return (x * 4 + yy * 2 + cc, z * 2 + c)

    def halves_of(n):
        if n % 2 == 0:
            return q_all.at[pl.ds(0, n // 2)]
        return spare.at[pl.ds(0, n)]

    def rows_of(n):
        return qn_all.at[pl.ds(0, n)]

    def sums_of(n):
        return xq_in.at[pl.ds(0, n)]

    room = {halves_of: 32, rows_of: 16, sums_of: 8}
    groups = []

    def send(build, when=None, size=1, kind=halves_of):
        for group in groups:
            if group["when"] is when and group["kind"] is kind and group["size"] + size <= room[kind]:
                break
        else:
            group = {"when": when, "kind": kind, "size": 0, "index": len(groups)}
            groups.append(group)
        group["size"] += size
        index = group["index"]

        def go():
            src, dst, rsem, to = build()
            pltpu.make_async_remote_copy(
                src_ref=src, dst_ref=dst, send_sem=ssem.at[index], recv_sem=rsem, device_id=to, device_id_type=MESH
            ).start()

        if when is None:
            go()
        else:
            pl.when(when)(go)

    def row(build, when=None):
        send(build, when, 1, rows_of)

    def wait(what, rsem):
        pltpu.make_async_remote_copy(
            src_ref=what, dst_ref=what, send_sem=lsem.at[0], recv_sem=rsem, device_id=partner, device_id_type=MESH
        ).wait_recv()

    def settle():
        assert len(groups) <= N_SENDS
        for group in groups:

            def done(group=group):
                what = group["kind"](group["size"])
                pltpu.make_async_remote_copy(
                    src_ref=what,
                    dst_ref=what,
                    send_sem=ssem.at[group["index"]],
                    recv_sem=lsem.at[0],
                    device_id=partner,
                    device_id_type=MESH,
                ).wait_send()

            if group["when"] is None:
                done()
            else:
                pl.when(group["when"])(done)

    me_q = c * 8 + z
    low, high = pl.ds(0, HALF), pl.ds(HALF, HALF)
    halves = (low, high)
    norms = pltpu.make_async_copy(qn_in, qn_smem, lsem.at[2])
    local_q = pltpu.make_async_copy(q_in, q_all.at[me_q], lsem.at[1])
    local_p = pltpu.make_async_copy(p_in, p_own, lsem.at[3])
    local_p.start()
    local_q.start()
    norms.start()
    barrier = pltpu.get_barrier_semaphore()
    peers = [at_x(2, cc) for cc in (0, 1)] + [at_y(2, cc) for cc in (0, 1)]
    peers += [at_x(d, cc) for d in (1, 3) for cc in (0, 1)]
    peers += [at_y(d, cc) for d in (1, 3) for cc in (0, 1)]
    peers += [at_z(d) for d in Z_PEERS]
    peers += [partner]
    for peer in peers:
        pl.semaphore_signal(barrier, inc=1, device_id=peer, device_id_type=MESH)

    @pl.when(same)
    def _():
        pltpu.make_async_copy(p_in, p_all.at[slab], lsem.at[4]).start()
        pltpu.make_async_copy(pn_in, pn_all.at[0], lsem.at[5]).start()

    local_p.wait()
    local_q.wait()
    pl.semaphore_wait(barrier, len(peers))

    def own(half, rsem, to, when=None):
        send(lambda: (p_own.at[half], p_all.at[slab, half], rsem, to), when)

    def q_half(slot, h, rsem, to):
        send(lambda: (q_all.at[slot, halves[h]], q_all.at[slot, halves[h]], rsem, to))

    def q_block(slot, rsem, to):
        send(lambda: (q_all.at[slot], q_all.at[slot], rsem, to), None, 2)

    def n_send(slot, rsem, to):
        row(lambda: (qn_all.at[slot], qn_all.at[slot], rsem, to))

    apart = jnp.logical_not(same)
    own(low, pa_sem.at[0], partner, apart)
    own(high, pb_sem.at[yl], partner, apart)
    q_half(me_q, 0, q_sem.at[2], at_z(2))
    q_half(me_q, 1, q_sem.at[5], at_z(6))
    for d in (1, 3):
        own(low, pa_sem.at[4 - d], at_x(d, yh))
        own(high, pb_sem.at[yl], at_y(d, yh))
    q_half(me_q, 1, q_sem.at[3], at_z(2))
    q_half(me_q, 0, q_sem.at[4], at_z(6))
    q_block(me_q, q_sem.at[0], at_z(1))
    q_block(me_q, q_sem.at[1], at_z(7))
    own(low, pa_sem.at[2], at_x(2, yh))
    own(high, pb_sem.at[yl], at_y(2, yh))
    for d in (1, 3, 2):
        own(low, pa_sem.at[4], at_y(d, c), same)
        own(high, pb_sem.at[2], at_x(d, c), same)
    q_block(me_q, q_sem.at[9], partner)

    @pl.when(same)
    def _():
        copy = pltpu.make_async_remote_copy(
            src_ref=pn_in,
            dst_ref=pn_all.at[0],
            send_sem=lsem.at[6],
            recv_sem=pn_sem.at[0],
            device_id=at_y(2, c),
            device_id_type=MESH,
        )
        copy.start()

    norms.wait()
    lanes = lax.broadcasted_iota(jnp.int32, (1, 128), 1)
    line = jnp.zeros((1, 128), F32)
    for i in range(ROWS):
        line = jnp.where(lanes == i, qn_smem[i], line)
    qn_all[me_q] = line
    for i, to in ((2, at_z(2)), (3, at_z(6)), (0, at_z(1)), (1, at_z(7)), (7, partner)):
        n_send(me_q, qn_sem.at[i], to)

    def relay_a(e, ccs):
        first = xs[e] * 4 + in_row

        @pl.when(same)
        def _():
            wait(halves_of(len(ccs)), pa_sem.at[e])

        for cc in ccs:
            slot = first + cc
            for d in (1, 3, 2):
                send(
                    lambda slot=slot, d=d: (p_all.at[slot, low], p_all.at[slot, low], pa_sem.at[4], at_y(d, c)), same
                )

    def relay_b(yy, ccs, when=None):
        def arrive():
            wait(halves_of(len(ccs)), pb_sem.at[yy])

        if when is None:
            arrive()
        else:
            pl.when(when)(arrive)
        for cc in ccs:
            slot = x * 4 + yy * 2 + cc
            for d in (1, 3, 2):
                send(
                    lambda slot=slot, d=d: (p_all.at[slot, high], p_all.at[slot, high], pb_sem.at[2], at_x(d, c)), when
                )

    relay_a(0, (other,))
    relay_b(yl, (other,), same)
    relay_a(1, (0, 1))
    relay_a(3, (0, 1))
    relay_b(yl, (0, 1), apart)
    relay_b(1 - yl, (0, 1))
    slots = {k: (c * 8 + zs[8 - k], c * 8 + zs[k]) for k in (1, 2, 3)}
    left, right = slots[2]
    wait(halves_of(1), q_sem.at[2])
    q_half(left, 0, q_sem.at[8], at_z(2))
    q_half(left, 0, q_sem.at[6], at_z(1))
    q_half(left, 0, q_sem.at[9], partner)
    wait(halves_of(1), q_sem.at[5])
    q_half(right, 1, q_sem.at[8], at_z(6))
    q_half(right, 1, q_sem.at[7], at_z(7))
    q_half(right, 1, q_sem.at[9], partner)
    relay_a(2, (0, 1))
    wait(halves_of(1), q_sem.at[3])
    q_half(left, 1, q_sem.at[6], at_z(1))
    q_half(left, 1, q_sem.at[9], partner)
    wait(halves_of(1), q_sem.at[4])
    q_half(right, 0, q_sem.at[7], at_z(7))
    q_half(right, 0, q_sem.at[9], partner)
    wait(rows_of(1), qn_sem.at[2])
    n_send(left, qn_sem.at[6], at_z(2))
    n_send(left, qn_sem.at[4], at_z(1))
    n_send(left, qn_sem.at[7], partner)
    wait(rows_of(1), qn_sem.at[3])
    n_send(right, qn_sem.at[5], at_z(7))
    n_send(right, qn_sem.at[7], partner)
    for i, slot in ((0, slots[1][0]), (1, slots[1][1]), (6, slots[3][0]), (7, slots[3][1]), (8, c * 8 + zs[4])):
        wait(halves_of(2), q_sem.at[i])
        q_block(slot, q_sem.at[9], partner)
        n = i if i < 2 else i - 2
        wait(rows_of(1), qn_sem.at[n])
        n_send(slot, qn_sem.at[7], partner)

    @pl.when(same)
    def _():
        wait(halves_of(8), pa_sem.at[4])
        pltpu.make_async_copy(p_in, p_all.at[slab], lsem.at[4]).wait()
        pltpu.make_async_copy(pn_in, pn_all.at[0], lsem.at[5]).wait()
        pltpu.make_async_remote_copy(
            src_ref=pn_in,
            dst_ref=pn_all.at[0],
            send_sem=lsem.at[6],
            recv_sem=pn_sem.at[0],
            device_id=at_y(2, c),
            device_id_type=MESH,
        ).wait_send()

    @pl.when(apart)
    def _():
        wait(halves_of(16), pa_sem.at[4])
        wait(pn_all.at[0], pn_sem.at[0])

    wait(halves_of(12), pb_sem.at[2])
    wait(halves_of(16), q_sem.at[9])
    wait(rows_of(8), qn_sem.at[7])

    scale = 2.0 / math.sqrt(width)
    columns = pn_all.shape[1]
    b = jnp.exp(TOP - pn_all[...])
    a_t = jnp.exp(TOP - qn_all[...].reshape(16, 128)).T
    passages = p_all[...].reshape(columns, width)
    largest = jnp.zeros((8, 128), F32)
    column = lax.broadcasted_iota(jnp.int32, (ROWS, columns), 1) - lax.broadcasted_iota(jnp.int32, (ROWS, columns), 0)
    for chunk in range(4):
        rows = q_all[pl.ds(chunk * 4, 4)].reshape(4 * ROWS, width)
        scores = lax.dot_general(rows, passages, (((1,), (1,)), ((), ())), preferred_element_type=F32)
        terms = jnp.exp2(scores * (scale * LOG2E) - TOP * LOG2E)
        for k in range(4):
            slot = chunk * 4 + k
            first = ((x * 4 + yl * 2 + slot // 8) * 16 + (slot % 8) * 2 + yh) * ROWS - (z * 2 + c) * columns
            here = slice(k * ROWS, (k + 1) * ROWS)
            weights = terms[here] * (a_t[:ROWS, slot : slot + 1] + b) - jnp.where(column == first, 2.0, 0.0)
            top = weights.astype(BF16)
            at = pl.ds(slot * ROWS, ROWS)
            w_hi[at, :] = top
            w_lo[at, :] = (weights - top.astype(F32)).astype(BF16)
            size = jnp.abs(weights)
            size = jnp.maximum(size[:HALF], size[HALF:])
            size = jnp.maximum(size[:8], size[8:])
            for j in range(columns // 128):
                largest = jnp.maximum(largest, size[:, j * 128 : (j + 1) * 128])
    mine = jnp.maximum(jnp.max(largest, axis=(0, 1), keepdims=True), 1e-30) * BOUND
    mine = jnp.broadcast_to(mine, (1, 128))
    sc_me[0] = mine
    row_of = [2 * c + yy for yy in (0, 1)]
    far_row = [row != y for row in row_of]
    back_a = [lax.rem(y - row + 3 + 4, 4) for row in row_of]
    back_b = [lax.rem(y - row + 4, 4) for row in row_of]
    row(lambda: (sc_me.at[0], sx_in.at[0], xs_sem.at[0], partner))
    for d in (2, 1, 3):
        row(lambda d=d: (sc_me.at[0], sx1_in.at[3 - d], rbs_sem.at[0], at_x(d, c)))
    for yy in (0, 1):
        row(
            lambda yy=yy: (sc_me.at[0], sy1_in.at[back_a[yy]], ras_sem.at[0], at_owner(yy, c)),
            far_row[yy],
        )

    def lane(row):
        return row[:, :1]

    inverse = lane(1.0 / mine)

    for chunk in range(2):
        at = pl.ds(pl.multiple_of(other * 8 * ROWS + chunk * 4 * ROWS, 4 * ROWS), 4 * ROWS)
        part = jnp.dot(w_hi[at, :], passages, preferred_element_type=F32)
        part += jnp.dot(w_lo[at, :], passages, preferred_element_type=F32)
        to = pl.ds(chunk * 4, 4)
        xq_out[to] = part.reshape(4, ROWS, width)
        send(lambda to=to: (xq_out.at[to], xq_in.at[to], xq_sem.at[0], partner), None, 4, sums_of)
    for chunk in range(2):
        at = pl.ds(pl.multiple_of(c * 8 * ROWS + chunk * 4 * ROWS, 4 * ROWS), 4 * ROWS)
        part = jnp.dot(w_hi[at, :], passages, preferred_element_type=F32)
        part += jnp.dot(w_lo[at, :], passages, preferred_element_type=F32)
        g_q[pl.ds(chunk * 4, 4)] = part.reshape(4, ROWS, width)

    queries = q_all[...].reshape(16 * ROWS, width)
    across = (((0,), (0,)), ((), ()))

    def passage_chunk(d):
        xm = xs[d]
        at = pl.ds(pl.multiple_of(xm * 4 * ROWS, 4 * ROWS), 4 * ROWS)
        part = lax.dot_general(w_hi[:, at], queries, across, preferred_element_type=F32)
        part += lax.dot_general(w_lo[:, at], queries, across, preferred_element_type=F32)
        part = part.reshape(2, 2, ROWS, width)
        g_p[xm] = part
        for yy in (0, 1):
            coded = encode(part[yy], inverse)
            pa_out[yy, xm] = coded[:, :HALF]
            if d:
                pb_out[3 - d, yy] = coded[:, HALF:]
                send(lambda yy=yy: (pb_out.at[3 - d, yy], pb_in.at[3 - d, yy], rb_sem.at[yy], at_x(d, c)), None, 2)
            send(
                lambda yy=yy: (pa_out.at[yy, xm], pa_in.at[back_a[yy], xm], ra_sem.at[xm], at_owner(yy, c)),
                far_row[yy],
                2,
            )

    passage_chunk(2)

    wait(rows_of(1), xs_sem.at[0])
    both = mine + sx_in[0]
    sc_q[0] = both
    wait(sums_of(8), xq_sem.at[0])
    for d in (1, 2, 6, 7):
        row(lambda d=d: (sc_q.at[0], sz_in.at[8 - d], zsc_sem.at[0], at_z(d)))
    inverse_q = lane(1.0 / both)

    def column_sum(zz):
        return g_q[zz] + xq_in[zz]

    far = encode(column_sum(zs[4]), inverse_q)
    zs1[4, low] = far[:HALF]
    zs1[4, high] = far[HALF:]
    for i, d in enumerate((5, 3)):
        zs1[i] = encode(column_sum(zs[d]), inverse_q)
    for i, d in enumerate((1, 7)):
        zs1[2 + i] = encode(column_sum(zs[d]), inverse_q)
    send(lambda: (zs1.at[4, low], zh_in.at[0], zr_sem.at[0], at_z(6)))
    send(lambda: (zs1.at[4, high], zh_in.at[1], zr_sem.at[1], at_z(2)))
    send(lambda: (zs1.at[0], zf_in.at[0], zr_sem.at[0], at_z(7)), None, 2)
    send(lambda: (zs1.at[1], zf_in.at[1], zr_sem.at[1], at_z(1)), None, 2)
    send(lambda: (zs1.at[2], zd_in.at[0], zd_sem.at[0], at_z(1)), None, 2)
    send(lambda: (zs1.at[3], zd_in.at[1], zd_sem.at[0], at_z(7)), None, 2)

    for d in (1, 3, 0):
        passage_chunk(d)

    def relay_rows():
        wait(rows_of(4), zsc_sem.at[0])
        for i in (0, 1):
            near, far_ = (1, 2) if i == 0 else (7, 6)
            to = at_z(6 if i == 0 else 2)
            wait(halves_of(3), zr_sem.at[i])
            total = both + sz_in[near] + sz_in[far_]
            sc_qr[i] = total
            value = column_sum(zs[6 if i == 0 else 2]) + decode(zf_in[i], lane(sz_in[near]))
            extra = decode(zh_in[i], lane(sz_in[far_]))
            inv = lane(1.0 / total)
            first_half, second_half = value[:HALF], value[HALF:]
            if i == 0:
                first_half = first_half + extra
            else:
                second_half = second_half + extra
            zs2[i, low] = encode(first_half, inv)
            zs2[i, high] = encode(second_half, inv)
            row(lambda i=i, to=to: (sc_qr.at[i], sz2_in.at[i], zsc2_sem.at[0], to))
            send(lambda i=i, to=to: (zs2.at[i], z2_in.at[i], z2_sem.at[0], to), None, 2)

    total_b = []

    def relay_upper(yy):
        if not total_b:
            wait(rows_of(3), rbs_sem.at[0])
            total_b.append(mine + sx1_in[0] + sx1_in[1] + sx1_in[2])
            sc_pb[0] = total_b[0]
        inv_b = lane(1.0 / total_b[0])
        wait(halves_of(6), rb_sem.at[yy])
        for cc in (0, 1):
            value = g_p[x, yy, cc, HALF:]
            for d in (2, 1, 3):
                value = value + decode(pb_in[d - 1, yy, cc], lane(sx1_in[d - 1]))
            fb_out[yy, cc] = encode(value, inv_b)
        for cc in (0, 1):
            mine_too = jnp.logical_and(jnp.logical_not(far_row[yy]), c == cc)

            @pl.when(mine_too)
            def _(cc=cc):
                fb_in[0] = fb_out[yy, cc]
                sfb_in[0] = total_b[0]

            away = jnp.logical_not(mine_too)
            back, to = back_b[yy], at_owner(yy, cc)
            row(lambda back=back, to=to: (sc_pb.at[0], sfb_in.at[back], fbs_sem.at[0], to), away)
            send(lambda cc=cc, back=back, to=to: (fb_out.at[yy, cc], fb_in.at[back], fb_sem.at[0], to), away)

    def relay_lower(e):
        xm = xs[e]

        @pl.when(same)
        def _():
            if e == 2:
                wait(rows_of(3), ras_sem.at[0])
                sc_pa[0] = mine + sy1_in[0] + sy1_in[1] + sy1_in[2]
            inv_a = lane(1.0 / sc_pa[0])
            wait(halves_of(6), ra_sem.at[xm])
            for cc in (0, 1):
                value = g_p[xm, yl, cc, :HALF]
                for d in (1, 2, 3):
                    value = value + decode(pa_in[d - 1, xm, cc], lane(sy1_in[d - 1]))
                fa_out[e, cc] = encode(value, inv_a)
            if e == 0:
                fa_in[0] = fa_out[0, c]
                sfa_in[0] = sc_pa[0]

        if e:
            back = 4 - e
            for cc in (0, 1):
                row(lambda cc=cc: (sc_pa.at[0], sfa_in.at[back], fas_sem.at[0], at_x(e, cc)), same)
                send(lambda cc=cc: (fa_out.at[e, cc], fa_in.at[back], fa_sem.at[0], at_x(e, cc)), same)
        else:
            row(lambda: (sc_pa.at[0], sfa_in.at[0], fas_sem.at[0], partner), same)
            send(lambda: (fa_out.at[0, other], fa_in.at[0], fa_sem.at[0], partner), same)

    relay_lower(2)
    relay_lower(1)
    relay_rows()
    relay_upper(0)
    relay_lower(3)
    relay_upper(1)
    relay_lower(0)

    value = column_sum(z)
    wait(halves_of(4), zd_sem.at[0])
    for i, d in ((0, 7), (1, 1)):
        value = value + decode(zd_in[i], lane(sz_in[d]))
    wait(rows_of(2), zsc2_sem.at[0])
    wait(halves_of(4), z2_sem.at[0])
    for i in (0, 1):
        value = value + decode(z2_in[i], lane(sz2_in[i]))
    oq_ref[...] = value

    for parts, scales, psem, sem, half in ((fb_in, sfb_in, fb_sem, fbs_sem, high), (fa_in, sfa_in, fa_sem, fas_sem, low)):
        for n, when in ((3, same), (4, apart)):

            @pl.when(when)
            def _(n=n, psem=psem, sem=sem):
                wait(rows_of(n), sem.at[0])
                wait(halves_of(n), psem.at[0])

        value = decode(parts[0], lane(scales[0]))
        for e in (1, 2, 3):
            value = value + decode(parts[e], lane(scales[e]))
        op_ref[half, :] = value

    settle()


N_SENDS = 28
Z_PEERS = (2, 6, 1, 7)
VMEM_LIMIT = 20 * 2**20


def local(queries, passages, query_lognorm, passage_lognorm, loss_cotangent):
    width = queries.shape[1]
    columns = passage_lognorm.shape[0]
    dma = pltpu.SemaphoreType.DMA
    vm = pltpu.VMEM
    scratch = [
        vm((16, ROWS, width), BF16), vm((16, ROWS, width), BF16), vm((ROWS, width), BF16), vm((16, 1, 128), F32), vm((1, columns), F32),
        vm((16 * ROWS, columns), BF16), vm((16 * ROWS, columns), BF16),
        vm((8, ROWS, width), F32), vm((4, 2, 2, ROWS, width), F32),
        vm((8, ROWS, width), F32), vm((8, ROWS, width), F32),
        vm((5, ROWS, width), BF16), vm((2, ROWS, width), BF16), vm((2, ROWS, width), BF16),
        vm((2, ROWS, width), BF16), vm((2, HALF, width), BF16), vm((2, ROWS, width), BF16),
        vm((2, 4, 2, HALF, width), BF16), vm((3, 4, 2, HALF, width), BF16),
        vm((3, 2, 2, HALF, width), BF16), vm((3, 2, 2, HALF, width), BF16),
        vm((4, 2, HALF, width), BF16), vm((4, HALF, width), BF16),
        vm((2, 2, HALF, width), BF16), vm((4, HALF, width), BF16),
        *[vm((n, 1, 128), F32) for n in (1, 1, 2, 1, 1, 1, 8, 2, 3, 3, 4, 4)],
        vm((8, HALF, width), BF16), pltpu.SMEM((ROWS,), F32), dma((N_SENDS,)), dma((7,)), dma((10,)), dma((8,)), dma((5,)), dma((3,)), dma((1,)),
        *[dma((n,)) for n in (1, 1, 1, 2, 1, 1, 1, 4, 2, 1, 1, 1, 1, 1, 1)],
    ]
    out = jax.ShapeDtypeStruct(queries.shape, F32)
    vmem = pl.BlockSpec(memory_space=pltpu.VMEM)

    def kernel(*refs):
        body(width, *refs)

    sums = pl.pallas_call(
        kernel,
        out_shape=(out, out),
        in_specs=[pl.BlockSpec(memory_space=pltpu.HBM)] * 4,
        out_specs=[vmem] * 2,
        scratch_shapes=scratch,
        compiler_params=pltpu.CompilerParams(collective_id=0, has_side_effects=True, vmem_limit_bytes=VMEM_LIMIT),
    )(*[pltpu.with_memory_space_constraint(v, pltpu.HBM) for v in (queries, passages, query_lognorm, passage_lognorm)])

    sums = lax.optimization_barrier((sums[0], sums[1], loss_cotangent))
    factor = sums[2] * (1.0 / math.sqrt(width))
    return sums[0] * factor, sums[1] * factor


def solution(mesh):
    return jax.shard_map(
        local,
        mesh=mesh,
        in_specs=(
            P(("slab", "blk"), None),
            P(("blk", "slab"), None),
            P(("slab", "blk")),
            P("blk"),
            P(),
        ),
        out_specs=(P(("slab", "blk"), None), P(("blk", "slab"), None)),
        check_vma=False,
    )
```

time: 37.7 us -> 36.3 us (0.963)
  Pallas kernels: 35.5 us -> 34.2 us
    pallas_call x1, Pallas kernels: 35.5 us -> 34.2 us  [local(): pl.pallas_call(kernel, out_shape=(out, out), in_specs=[pl.BlockSpec(memor...]
where the time goes in v4:
time: 36.3 us; the launch traced here: 36.2 us
  Pallas kernels  34.2 us (94%)
  between operations  1.29 us (4%)
  other arithmetic  0.69 us (2%)
    pallas_call x1, Pallas kernels, local(): pl.pallas_call(kernel, out_shape=(out, out), in_specs=[pl.BlockSpec(memor...  34.2 us

profile of v4, /device:TPU:1, one launch (start us, length us, event | category | flops | bytes accessed | tf_op | source)
XLA Modules:
  0.0 36.2 jit_solution(12848942773607682836)
XLA Ops:
  1.3 34.2 %shard_map.68 = (f32[32,768]{1,0:T(8,128)S(1)}, f32[32,768]{1,0:T(8,128)S(1)}) custom-call(bf16[32,768]{1,0:T(8,128)(2,1)} %refs_0_.1, bf16[32,768]{1,0:T(8,128)(2,1)} %refs_1_.1, f32[32]{0:T(128)} %refs_2_.1, f32[512]{0:T(512)} %refs_3_.1), custom_call_target="tpu_custom_call" | custom-call | tf_op jit(solution)/shard_map/pallas_call | solution.py:558
  35.5 0.7 %broadcast_multiply_fusion = (f32[32,768]{1,0:T(8,128)}, f32[32,768]{1,0:T(8,128)}) fusion(f32[32,768]{1,0:T(8,128)S(1)} %get-tuple-element.11, f32[]{:T(128)S(6)} %mul.13, f32[32,768]{1,0:T(8,128)S(1)} %get-tuple-element.9), kind=kLoop, calls=%fused_computation | loop fusion | flops 49152 | bytes 393220 | tf_op jit(solution)/shard_map/mul | solution.py:569

commit v5 on v4

--- a/solution.py
+++ b/solution.py
@@ -385,6 +385,7 @@
             )
 
     passage_chunk(2)
+    passage_chunk(1)
 
     wait(rows_of(1), xs_sem.at[0])
     both = mine + sx_in[0]
@@ -411,7 +412,7 @@
     send(lambda: (zs1.at[2], zd_in.at[0], zd_sem.at[0], at_z(1)), None, 2)
     send(lambda: (zs1.at[3], zd_in.at[1], zd_sem.at[0], at_z(7)), None, 2)
 
-    for d in (1, 3, 0):
+    for d in (3, 0):
         passage_chunk(d)
 
     def relay_rows():
@@ -524,7 +525,7 @@
     settle()
 
 
-N_SENDS = 28
+N_SENDS = 22
 Z_PEERS = (2, 6, 1, 7)
 VMEM_LIMIT = 20 * 2**20
 

time: 36.3 us -> 36.4 us (level)
  no operation moved by 1% of the time
where the time goes in v5:
time: 36.4 us; the launch traced here: 36.2 us
  Pallas kernels  34.3 us (94%)
  between operations  1.29 us (4%)
  other arithmetic  0.69 us (2%)
    pallas_call x1, Pallas kernels, local(): pl.pallas_call(kernel, out_shape=(out, out), in_specs=[pl.BlockSpec(memor...  34.3 us

profile of v5, /device:TPU:1, one launch (start us, length us, event | category | flops | bytes accessed | tf_op | source)
XLA Modules:
  0.0 36.2 jit_solution(16352449828906430006)
XLA Ops:
  1.3 34.3 %shard_map.68 = (f32[32,768]{1,0:T(8,128)S(1)}, f32[32,768]{1,0:T(8,128)S(1)}) custom-call(bf16[32,768]{1,0:T(8,128)(2,1)} %refs_0_.1, bf16[32,768]{1,0:T(8,128)(2,1)} %refs_1_.1, f32[32]{0:T(128)} %refs_2_.1, f32[512]{0:T(512)} %refs_3_.1), custom_call_target="tpu_custom_call" | custom-call | tf_op jit(solution)/shard_map/pallas_call | solution.py:559
  35.6 0.7 %broadcast_multiply_fusion = (f32[32,768]{1,0:T(8,128)}, f32[32,768]{1,0:T(8,128)}) fusion(f32[32,768]{1,0:T(8,128)S(1)} %get-tuple-element.11, f32[]{:T(128)S(6)} %mul.13, f32[32,768]{1,0:T(8,128)S(1)} %get-tuple-element.9), kind=kLoop, calls=%fused_computation | loop fusion | flops 49152 | bytes 393220 | tf_op jit(solution)/shard_map/mul | solution.py:570
